TPU v7x, 512 devices: a whole 4x8x8 slice. The times are simulated.
512 devices in a mesh: group: 2 (over core), dp: 64 (over y, z), mp: 4 (over x).
Axes of the slice: x: 4, y: 8, z: 8, core: 2. Of those that a mesh axis runs over, the one named last changes fastest.
Arguments:
- kv_up_grads: bfloat16 [65536, 4096], P(('group', 'dp'), 'mp'), may hold values from -40 to 40
- tok_grads: bfloat16 [32768, 2048], P(('group', 'dp')), may hold values from -6 to 6
- token_rows: int32 [32768], P(('group', 'dp')), may hold values from 0 to 511
- step_count: int32 [1], replicated, may hold values from 1 to 11
- master: float32 [4, 786432], P('mp', 'dp'), may hold values from -0.12 to 0.12
- moment_one: float32 [4, 786432], P('mp', 'dp'), may hold values from -0.004 to 0.004
- moment_two: float32 [4, 786432], P('mp', 'dp'), may hold values from 1e-08 to 1e-06
- average: float32 [4, 786432], P('mp', 'dp'), may hold values from -0.12 to 0.12
Outputs:
- new_kv_up: bfloat16 [512, 4096], P(None, 'mp')
- new_embed: bfloat16 [512, 2048], P('mp')
- new_master: float32 [4, 786432], P('mp', 'dp')
- new_moment_one: float32 [4, 786432], P('mp', 'dp')
- new_moment_two: float32 [4, 786432], P('mp', 'dp')
- new_average: float32 [4, 786432], P('mp', 'dp')
All inputs are finite; a program needn't handle non-finite values.
Results may differ from a plain program's by a relative error of at most 0.001.
Values may be sent and summed in bfloat16 or wider, within the bound.
A program may use at most 64 MiB of HBM per device.

v0:
```python
import jax
import jax.numpy as jnp
from jax import lax
from jax.sharding import PartitionSpec as P

EROWS = 512


BETA_ONE = 0.9
BETA_TWO = 0.95
LEARN_RATE = 0.02
DECAY_RATE = 0.1
EPSILON = 1e-08
CLIP_NORM = 1.0
AVG_DECAY = 0.9


def shards(kv_up_grads, tok_grads, token_rows, step_count, master, moment_one, moment_two, average):
    block_rows = EROWS // lax.axis_size("mp")
    row_start = lax.axis_index("mp") * block_rows
    slot_ids = row_start + lax.iota(jnp.int32, block_rows)
    onehot = (slot_ids[:, None] == token_rows[None, :]).astype(jnp.bfloat16)
    embed_part = jnp.dot(onehot, tok_grads, preferred_element_type=jnp.float32)
    latent_part = kv_up_grads.astype(jnp.float32)
    latent_rows, embed_rows = (
        lax.psum_scatter(latent_part, "dp", scatter_dimension=0, tiled=True),
        lax.psum_scatter(embed_part, "dp", scatter_dimension=0, tiled=True),
    )
    latent_rows, embed_rows = lax.psum((latent_rows, embed_rows), "group")
    gradient = jnp.concatenate([latent_rows.reshape(1, -1), embed_rows.reshape(1, -1)], axis=1)
    sum_squares = lax.psum(jnp.sum(gradient * gradient), ("dp", "mp"))
    norm_value = jnp.sqrt(sum_squares)
    factor = CLIP_NORM / jnp.maximum(norm_value, CLIP_NORM)
    clipped = factor * gradient
    step_float = step_count[0].astype(jnp.float32)
    new_moment_one = BETA_ONE * moment_one + (1.0 - BETA_ONE) * clipped
    new_moment_two = BETA_TWO * moment_two + (1.0 - BETA_TWO) * clipped * clipped
    first_hat = new_moment_one / (1.0 - jnp.power(jnp.float32(BETA_ONE), step_float))
    second_hat = new_moment_two / (1.0 - jnp.power(jnp.float32(BETA_TWO), step_float))
    new_master = master - LEARN_RATE * (
        first_hat / (jnp.sqrt(second_hat) + EPSILON) + DECAY_RATE * master
    )
    new_average = AVG_DECAY * average + (1.0 - AVG_DECAY) * new_master
    weights = new_master.astype(jnp.bfloat16)
    latent_len = latent_rows.shape[0] * latent_rows.shape[1]
    latent_new = weights[0, :latent_len].reshape(latent_rows.shape)
    embed_new = weights[0, latent_len:].reshape(embed_rows.shape)
    new_kv_up, new_embed = (
        lax.all_gather(latent_new, "dp", axis=0, tiled=True),
        lax.all_gather(embed_new, "dp", axis=0, tiled=True),
    )
    return (new_kv_up, new_embed, new_master, new_moment_one, new_moment_two, new_average)


def solution(mesh):
    placed = (
        P(("group", "dp"), "mp"),
        P(("group", "dp"), None),
        P(("group", "dp")),
        P(),
        P("mp", "dp"),
        P("mp", "dp"),
        P("mp", "dp"),
        P("mp", "dp"),
    )
    return jax.shard_map(
        shards,
        mesh=mesh,
        in_specs=placed,
        out_specs=(
            P(None, "mp"),
            P("mp", None),
            P("mp", "dp"),
            P("mp", "dp"),
            P("mp", "dp"),
            P("mp", "dp"),
        ),
        check_vma=False,
    )
```

profile of v0, /device:TPU:1, one launch (start us, length us, event | category | flops | bytes accessed | tf_op | source)
XLA Modules:
  0.0 1094.9 jit_solution(456256564318343173)
XLA Ops:
  7.2 0.0 copy-start
  7.2 0.0 all-reduce.6.cloned.1.call-start
  7.2 1.2 copy-done
  8.4 2.0 fusion
  10.4 0.0 copy-start.2
  10.4 0.0 copy-start.3
  10.4 0.0 copy-start.4
  10.4 0.0 copy-start.5
  10.4 0.0 all-reduce.6.cloned.1.call-update
  10.4 0.0 all-gather.3.cloned.1.call-start
  10.5 1.3 dynamic-slice
  12.4 255.5 %all-reduce.7 = f32[512,1024]{1,0:T(8,128)S(1)} all-reduce(bf16[512,1024]{1,0:T(8,128)(2,1)} %param.8), channel_id=2, replica_groups=mesh['group'=2,'dp'=64,'mp'=4] {'dp'}, use_global_device_ids=true, to_apply=%region_0.0.clone | all-reduce | flops 524288 | bytes 3145728
  269.4 0.0 all-reduce.6.cloned.1.call-done
  269.4 0.9 dynamic-slice_bitcast_fusion.1
  270.3 58.7 %all-reduce.2 = (f32[1,8192]{1,0:T(1,128)S(1)}, f32[1,4096]{1,0:T(1,128)S(1)}) all-reduce(f32[1,8192]{1,0:T(1,128)S(1)} %bitcast.12, f32[1,4096]{1,0:T(1,128)S(1)} %bitcast.13), channel_id=1, replica_groups=mesh['group'=2,'dp'=64,'mp'=4] {'group'}, use_global_device_ids=true, to_apply=%region_1.0 | all-reduce | flops 12288 | bytes 98304 | tf_op jit(solution)/shard_map/psum | solution.py:29
  329.0 0.7 multiply_reduce_fusion
  329.7 575.6 %psum.23 = f32[]{:T(128)} all-reduce(f32[]{:T(128)} %multiply_reduce_fusion), channel_id=1, replica_groups=mesh['group'=2,'dp'=64,'mp'=4] {'dp','mp'}, use_global_device_ids=true, to_apply=%region_5.0 | all-reduce | flops 1 | bytes 8 | tf_op jit(solution)/shard_map/psum | solution.py:31
  906.0 0.0 copy-done.2
  906.0 0.0 copy-done.3
  906.1 0.0 copy-done.4
  906.1 0.0 copy-done.5
  906.1 1.0 multiply_add_fusion
  907.1 0.0 copy-start.1
  907.1 0.1 slice_reduce_fusion
  907.2 0.6 reshape_squeeze.6
  907.8 0.0 all-gather.3.cloned.1.call-update
  907.9 0.1 slice_reduce_fusion.1
  907.9 36.6 %all-gather = bf16[64,2,2048]{2,1,0:T(2,128)(2,1)S(1)} all-gather(bf16[1,2,2048]{2,1,0:T(2,128)(2,1)S(1)} %reshape.128), channel_id=1, replica_groups=mesh['group'=2,'dp'=64,'mp'=4] {'dp'}, dimensions={0}, use_global_device_ids=true | all-gather | bytes 532480 | tf_op jit(solution)/shard_map/all_gather | solution.py:50
  944.5 1.0 reshape.129
  945.5 140.3 %all-gather.3.cloned.1.call-done = bf16[512,1024]{1,0:T(8,128)(2,1)} async-done(((bf16[8,1024]{1,0:T(8,128)(2,1)}), bf16[512,1024]{1,0:T(8,128)(2,1)}) %all-gather.3.cloned.1.call-update) | async-done | bytes 1048592 | tf_op jit(solution)/shard_map/all_gather | solution.py:49
  1085.8 2.3 copy.22
  1088.1 0.0 copy-done.1
  (8 shorter events, 0.1 us)
Async XLA Ops:
  7.2 1.2 copy-start
  7.2 262.2 %all-reduce.6.cloned.1.call-start = ((), (), s32[]{:S(2)}) async-start(), calls=%async_computation.1 | async-start | bytes 2097152
  10.4 895.6 %copy-start.2 = (f32[1,12288]{1,0:T(1,128)S(1)}, f32[1,12288]{1,0:T(1,128)}, u32[]{:S(2)}) copy-start(f32[1,12288]{1,0:T(1,128)} %param.15) | copy-start | bytes 147460
  10.4 895.6 %copy-start.3 = (f32[1,12288]{1,0:T(1,128)S(1)}, f32[1,12288]{1,0:T(1,128)}, u32[]{:S(2)}) copy-start(f32[1,12288]{1,0:T(1,128)} %param.12) | copy-start | bytes 147460
  10.4 895.7 %copy-start.4 = (f32[1,12288]{1,0:T(1,128)S(1)}, f32[1,12288]{1,0:T(1,128)}, u32[]{:S(2)}) copy-start(f32[1,12288]{1,0:T(1,128)} %param.14) | copy-start | bytes 147460
  10.4 895.7 %copy-start.5 = (f32[1,12288]{1,0:T(1,128)S(1)}, f32[1,12288]{1,0:T(1,128)}, u32[]{:S(2)}) copy-start(f32[1,12288]{1,0:T(1,128)} %param.13) | copy-start | bytes 147460
  10.4 1075.4 %all-gather.3.cloned.1.call-start = ((), (), s32[]{:S(2)}) async-start(), calls=%async_computation | async-start | bytes 1064960 | tf_op jit(solution)/shard_map/all_gather | solution.py:49
  907.1 181.0 %copy-start.1 = (f32[1,12288]{1,0:T(1,128)}, f32[1,12288]{1,0:T(1,128)S(1)}, u32[]{:S(2)}) copy-start(f32[1,12288]{1,0:T(1,128)S(1)} %get-tuple-element.20) | copy-start | bytes 147460
Sparse Core Ops, SparseCore 0:
  11.8 162.4 all-reduce.5
  908.0 177.7 all-gather.2
where the time goes:
time: 1100 us; the launch traced here: 1090 us
  blocking collectives  926 us (84%)
  waiting for transfers between devices  140 us (13%)
  between operations  16.9 us (2%)
    psum x1, blocking collectives, shards(): sum_squares = lax.psum(jnp.sum(gradient * gradient), ('dp', 'mp'))  576 us
    unnamed x1, blocking collectives  256 us
    all_gather x1, waiting for transfers between devices, shards(): lax.all_gather(latent_new, 'dp', axis=0, tiled=True)  140 us
    psum x1, blocking collectives, shards(): latent_rows, embed_rows = lax.psum((latent_rows, embed_rows), 'group')  58.7 us
    all_gather x1, blocking collectives, shards(): lax.all_gather(embed_new, 'dp', axis=0, tiled=True)  36.6 us
  transfers between devices with their start and end apart: 2, of which 1 were waited for; matrix products, arithmetic and copies ran while one was open for 0% of the time, Pallas kernels for 0%

commit v1 on v0

v1 whole, which is shorter than its diff:
```python
import math

import jax
import jax.numpy as jnp
import numpy as np
from jax import lax
from jax.experimental import pallas as pl
from jax.experimental.pallas import tpu as pltpu
from jax.sharding import PartitionSpec as P

BETA_ONE = 0.9
BETA_TWO = 0.95
LEARN_RATE = 0.02
DECAY_RATE = 0.1
EPSILON = 1e-08
CLIP_NORM = 1.0
AVG_DECAY = 0.9

MESH = pl.DeviceIdType.MESH
LANES = 128
ROWS = 8


def step_kernel(
    n, nx, cols, width,
    kv, tok, trow, step, master, moment_one, moment_two, average,
    okv, oem, omaster, omoment_one, omoment_two, oaverage,
    kvbuf, toks, rows, part, embuf, share, share_in, grads, state,
    norm_a, norm_b, norm_c, wem,
    state_sem, local_sem, tok_sem, kv_send, kv_recv, em_send, em_recv,
    s2_send, s2_recv, g_sem, na_send, na_recv, nb_send, nb_recv, nc_send, nc_recv,
    ga_send, ga_recv, gb_send, gb_recv, gc_send, gc_recv,
):
    group = lax.axis_index("group")
    owner = lax.axis_index("dp")
    block = lax.axis_index("mp")
    y, z = owner // n, owner % n
    other = 1 - group
    half, ehalf = cols // 2, width // 2
    chunks, echunks = half // LANES, ehalf // LANES
    one = y * other + z * group
    two = z * other + y * group

    def along_y(place):
        return place * n + z

    def along_z(place):
        return y * n + place

    def along_one(place):
        return along_y(place) * other + along_z(place) * group

    def along_two(place):
        return along_z(place) * other + along_y(place) * group

    def each(body):
        def wrapped(k, _):
            body(k)
            return 0

        lax.fori_loop(1, n, wrapped, 0)

    def remote(src, dst, send, recv, device):
        return pltpu.make_async_remote_copy(
            src_ref=src, dst_ref=dst, send_sem=send, recv_sem=recv, device_id=device, device_id_type=MESH
        )

    states = [
        pltpu.make_async_copy(ref, state.at[i], state_sem.at[i])
        for i, ref in enumerate((master, moment_one, moment_two, average))
    ]
    for copy in states:
        copy.start()

    ecols = pl.ds(pl.multiple_of(group * ehalf, ehalf), ehalf)
    ecols_other = pl.ds(pl.multiple_of(other * ehalf, ehalf), ehalf)
    tok_here = pltpu.make_async_copy(tok.at[:, ecols], toks.at[group], local_sem.at[1])
    row_here = pltpu.make_async_copy(trow, rows.at[group], local_sem.at[2])
    tok_here.start()
    row_here.start()

    barrier = pltpu.get_barrier_semaphore()

    def greet(k):
        for core in range(2):
            pl.semaphore_signal(barrier, inc=1, device_id=(core, along_y((y + k) % n), block), device_id_type=MESH)
            pl.semaphore_signal(barrier, inc=1, device_id=(core, along_z((z + k) % n), block), device_id_type=MESH)

    each(greet)
    for k in range(1, nx):
        for core in range(2):
            pl.semaphore_signal(barrier, inc=1, device_id=(core, owner, (block + k) % nx), device_id_type=MESH)
    pl.semaphore_signal(barrier, inc=1, device_id=(other, owner, block), device_id_type=MESH)
    pl.semaphore_wait(barrier, 4 * (n - 1) + 2 * (nx - 1) + 1)

    partner = (other, owner, block)
    tok_there = remote(tok.at[:, ecols_other], toks.at[group], tok_sem.at[0], tok_sem.at[1], partner)
    row_there = remote(trow, rows.at[group], tok_sem.at[2], tok_sem.at[3], partner)
    tok_there.start()
    row_there.start()

    def kv_first(place):
        return kv.at[place, :, :, pl.ds(0, half)]

    def kv_second(place):
        return kv.at[:, place, :, pl.ds(half, half)]

    def send_first(k):
        place = (y + k) % n
        return remote(kv_first(place), kvbuf.at[group, y], kv_send.at[0, k], kv_recv.at[group, y], (0, along_y(place), block))

    def send_second(k):
        place = (z + k) % n
        return remote(kv_second(place), kvbuf.at[group, z], kv_send.at[1, k], kv_recv.at[group, z], (1, along_z(place), block))

    def start_kv(k):
        send_first(k).start()
        send_second(k).start()

    keep_first = pltpu.make_async_copy(kv_first(y), kvbuf.at[group, y], local_sem.at[0])
    keep_second = pltpu.make_async_copy(kv_second(z), kvbuf.at[group, z], local_sem.at[0])
    pass_first = remote(kv_first(y), kvbuf.at[group, y], kv_send.at[0, 0], kv_recv.at[group, y], partner)
    pass_second = remote(kv_second(z), kvbuf.at[group, z], kv_send.at[0, 0], kv_recv.at[group, z], partner)

    each(start_kv)

    @pl.when(group == 0)
    def _():
        keep_first.start()
        pass_second.start()

    @pl.when(group == 1)
    def _():
        keep_second.start()
        pass_first.start()

    tok_here.wait()
    row_here.wait()
    tok_there.wait_recv()
    row_there.wait_recv()
    index = lax.broadcasted_iota(jnp.int32, (2 * n * n, 1), 0)
    first, second, pair = index // (2 * n), index % n, (index // n) % 2
    yy = first * other + second * group
    zz = second * other + first * group
    wanted = block * (2 * n * n) + 2 * (yy * n + zz) + pair
    total = jnp.zeros((2 * n * n, ehalf), jnp.float32)
    for core in range(2):
        onehot = jnp.where(wanted == rows[core], 1.0, 0.0).astype(jnp.bfloat16)
        total = total + jnp.dot(onehot, toks[core], preferred_element_type=jnp.float32)
    part[...] = total.reshape(n, 2 * n, ehalf)

    def send_em(k):
        place = (one + k) % n
        return remote(part.at[place], embuf.at[one], em_send.at[k], em_recv.at[one], (group, along_one(place), block))

    each(lambda k: send_em(k).start())
    embuf[one] = part[one]

    def wait_kv(k):
        place = (one + k) % n
        for core in range(2):
            remote(kvbuf.at[core, place], kvbuf.at[core, place], kv_send.at[0, 0], kv_recv.at[core, place], partner).wait_recv()

    each(wait_kv)
    remote(kvbuf.at[other, one], kvbuf.at[other, one], kv_send.at[0, 0], kv_recv.at[other, one], partner).wait_recv()
    keep_first.wait()

    def wait_em(k):
        place = (one + k) % n
        remote(part.at[0], embuf.at[place], em_send.at[0], em_recv.at[place], partner).wait_recv()

    each(wait_em)

    for c in range(echunks):
        span = pl.ds(c * LANES, LANES)
        for i in range(2):
            piece = embuf[0, pl.ds(i * n, n), span]
            for place in range(1, n):
                piece = piece + embuf[place, pl.ds(i * n, n), span]
            share[chunks + i, pl.ds(c, n, stride=ROWS), :] = piece

    def sum_kv(place):
        at = pl.ds(pl.multiple_of(place * ROWS, ROWS), ROWS)
        for c in range(chunks):
            span = pl.ds(c * LANES, LANES)
            acc = jnp.zeros((ROWS, LANES), jnp.float32)
            for core in range(2):
                for source in range(n):
                    acc = acc + kvbuf[core, source, place, :, span].astype(jnp.float32)
            share[c, at, :] = acc

    def send_share(k):
        place = (two + k) % n
        return remote(
            share.at[:, pl.ds(pl.multiple_of(place * ROWS, ROWS), ROWS), :],
            share_in.at[two], s2_send.at[k], s2_recv.at[two], (group, along_two(place), block),
        )

    def sum_and_send(k):
        sum_kv((two + k) % n)
        send_share(k).start()

    each(sum_and_send)
    sum_kv(two)
    share_in[two] = share[:, pl.ds(pl.multiple_of(two * ROWS, ROWS), ROWS), :]

    def wait_share(k):
        place = (two + k) % n
        remote(share_in.at[place], share_in.at[place], s2_send.at[0], s2_recv.at[place], partner).wait_recv()

    each(wait_share)
    mine = share_in[0]
    for place in range(1, n):
        mine = mine + share_in[place]
    grads[group] = mine
    swap = remote(grads.at[group], grads.at[group], g_sem.at[0], g_sem.at[1], partner)
    swap.start()

    squares = mine * mine
    lanes = squares[0]
    for c in range(1, chunks + 2):
        lanes = lanes + squares[c]
    norm_a[y] = jnp.sum(lanes, axis=0, keepdims=True)

    def send_a(k):
        place = (y + k) % n
        return remote(norm_a.at[y], norm_a.at[y], na_send.at[k], na_recv.at[y], (group, along_y(place), block))

    def wait_a(k):
        place = (y + k) % n
        remote(norm_a.at[place], norm_a.at[place], na_send.at[0], na_recv.at[place], partner).wait_recv()

    each(lambda k: send_a(k).start())
    each(wait_a)
    partial = norm_a[0]
    for place in range(1, n):
        partial = partial + norm_a[place]
    norm_b[z] = partial

    def send_b(k):
        place = (z + k) % n
        return remote(norm_b.at[z], norm_b.at[z], nb_send.at[k], nb_recv.at[z], (group, along_z(place), block))

    def wait_b(k):
        place = (z + k) % n
        remote(norm_b.at[place], norm_b.at[place], nb_send.at[0], nb_recv.at[place], partner).wait_recv()

    each(lambda k: send_b(k).start())
    each(wait_b)
    partial = norm_b[0]
    for place in range(1, n):
        partial = partial + norm_b[place]
    norm_c[group, block] = partial

    def send_c(k, core):
        place = (block + k) % nx
        to = group if core == 0 else other
        slot = 2 * k + core
        return remote(
            norm_c.at[group, block], norm_c.at[group, block], nc_send.at[slot], nc_recv.at[group, block], (to, owner, place)
        )

    fan = [(k, core) for k in range(nx) for core in range(2) if k or core]
    for k, core in fan:
        send_c(k, core).start()
    for k, core in fan:
        place = (block + k) % nx
        source = group if core == 0 else other
        remote(
            norm_c.at[source, place], norm_c.at[source, place], nc_send.at[0], nc_recv.at[source, place], partner
        ).wait_recv()
    partial = jnp.zeros((1, LANES), jnp.float32)
    for core in range(2):
        for place in range(nx):
            partial = partial + norm_c[core, place]
    norm_value = jnp.sqrt(jnp.sum(partial, axis=1, keepdims=True))
    factor = CLIP_NORM / jnp.maximum(norm_value, CLIP_NORM)

    swap.wait_recv()
    for copy in states:
        copy.wait()

    step_float = jnp.full((1, LANES), step[0], jnp.int32).astype(jnp.float32)
    one_scale = 1.0 - jnp.exp(step_float * math.log(np.float32(BETA_ONE)))
    two_scale = 1.0 - jnp.exp(step_float * math.log(np.float32(BETA_TWO)))

    def update(at, gradient):
        clipped = factor * gradient
        weight = state[0, at, :]
        new_one = BETA_ONE * state[1, at, :] + (1.0 - BETA_ONE) * clipped
        new_two = BETA_TWO * state[2, at, :] + (1.0 - BETA_TWO) * clipped * clipped
        first_hat = new_one / one_scale
        second_hat = new_two / two_scale
        new_weight = weight - LEARN_RATE * (first_hat / (jnp.sqrt(second_hat) + EPSILON) + DECAY_RATE * weight)
        omaster[at, :] = new_weight
        omoment_one[at, :] = new_one
        omoment_two[at, :] = new_two
        oaverage[at, :] = AVG_DECAY * state[3, at, :] + (1.0 - AVG_DECAY) * new_weight
        return new_weight

    row_chunks = cols // LANES
    for h in range(2):
        for c in range(chunks):
            span = pl.ds(h * half + c * LANES, LANES)
            new = update(pl.ds(h * chunks + c, ROWS, stride=row_chunks), grads[h, c])

            @pl.when(group == h)
            def _(new=new, span=span):
                okv[y, z, :, span] = new.astype(jnp.bfloat16)

        for i in range(2):
            at = pl.ds(ROWS * row_chunks + (i * 2 + h) * echunks, echunks)
            wem[h, pl.ds(i * echunks, echunks), :] = update(at, grads[h, chunks + i, 0:echunks, :])

    for c in range(echunks):
        for h in range(2):
            @pl.when(group == h)
            def _(h=h, c=c):
                oem[y, z, :, pl.ds(h * ehalf + c * LANES, LANES)] = wem[h, pl.ds(c, 2, stride=echunks), :].astype(jnp.bfloat16)

    kcols = pl.ds(pl.multiple_of(group * half, half), half)

    def gather_one(ref, span, kind, k):
        place = (one + k) % n
        here = ref.at[y, z, :, span]
        return remote(here, here, ga_send.at[kind, k], ga_recv.at[kind, one], (group, along_one(place), block))

    def send_ga(k):
        gather_one(okv, kcols, 0, k).start()
        gather_one(oem, ecols, 1, k).start()

    each(send_ga)

    def wait_ga(k):
        place = (one + k) % n
        for kind, ref, span in ((0, okv, kcols), (1, oem, ecols)):
            here = ref.at[y, z, :, span]
            remote(here, here, ga_send.at[kind, 0], ga_recv.at[kind, place], partner).wait_recv()

    each(wait_ga)

    def line(ref, core, place):
        if core == 0:
            return ref.at[:, place, :, pl.ds(0, ref.shape[3] // 2)]
        return ref.at[place, :, :, pl.ds(ref.shape[3] // 2, ref.shape[3] // 2)]

    def gather_two(core, kind, ref, k):
        place = (two + k) % n
        here = line(ref, core, two)
        return remote(here, here, gb_send.at[kind, k], gb_recv.at[kind, two], (core, along_two(place), block))

    def hand_over(core, kind, ref, place):
        here = line(ref, core, place)
        return remote(here, here, gc_send.at[kind, place], gc_recv.at[kind, place], partner)

    for core in range(2):
        @pl.when(group == core)
        def _(core=core):
            outs = ((0, okv), (1, oem))

            def send_gb(k):
                for kind, ref in outs:
                    gather_two(core, kind, ref, k).start()

            each(send_gb)
            for kind, ref in outs:
                hand_over(core, kind, ref, two).start()

            def pass_on(k):
                place = (two + k) % n
                for kind, ref in outs:
                    here = line(ref, core, place)
                    remote(here, here, gb_send.at[kind, 0], gb_recv.at[kind, place], partner).wait_recv()
                    hand_over(core, kind, ref, place).start()

            each(pass_on)

            def finish(place, _):
                for kind, ref in outs:
                    hand_over(1 - core, kind, ref, place).wait_recv()
                    hand_over(core, kind, ref, place).wait_send()
                return 0

            lax.fori_loop(0, n, finish, 0)

            def sent_gb(k):
                for kind, ref in outs:
                    gather_two(core, kind, ref, k).wait_send()

            each(sent_gb)

    tok_there.wait_send()
    row_there.wait_send()
    pass_first.wait_send()
    swap.wait_send()

    def sent(k):
        send_first(k).wait_send()
        send_second(k).wait_send()
        send_em(k).wait_send()
        send_share(k).wait_send()
        send_a(k).wait_send()
        send_b(k).wait_send()
        gather_one(okv, kcols, 0, k).wait_send()
        gather_one(oem, ecols, 1, k).wait_send()

    each(sent)
    for k, core in fan:
        send_c(k, core).wait_send()


def solution(mesh):
    owners, blocks = mesh.shape["dp"], mesh.shape["mp"]
    n = math.isqrt(owners)

    def shards(kv_up_grads, tok_grads, token_rows, step_count, master, moment_one, moment_two, average):
        cols, width, tokens = kv_up_grads.shape[1], tok_grads.shape[1], tok_grads.shape[0]
        rows = master.shape[1] // LANES
        half, ehalf = cols // 2, width // 2
        lines = lambda array: array.reshape(rows, LANES)
        dma, f32, bf16 = pltpu.SemaphoreType.DMA, jnp.float32, jnp.bfloat16
        any_space = pl.BlockSpec(memory_space=pltpu.HBM)
        vmem = pl.BlockSpec(memory_space=pltpu.VMEM)
        state = jax.ShapeDtypeStruct((rows, LANES), f32)
        share = half // LANES + 2

        def body(*refs):
            step_kernel(n, blocks, cols, width, *refs)

        outs = pl.pallas_call(
            body,
            out_shape=(
                jax.ShapeDtypeStruct((n, n, ROWS, cols), bf16),
                jax.ShapeDtypeStruct((n, n, 2, width), bf16),
                state, state, state, state,
            ),
            in_specs=[any_space] * 3 + [pl.BlockSpec(memory_space=pltpu.SMEM)] + [any_space] * 4,
            out_specs=[vmem] * 6,
            scratch_shapes=[
                pltpu.VMEM((2, n, n, ROWS, half), bf16),
                pltpu.VMEM((2, tokens, ehalf), bf16),
                pltpu.VMEM((2, 1, tokens), jnp.int32),
                pltpu.VMEM((n, 2 * n, ehalf), f32),
                pltpu.VMEM((n, 2 * n, ehalf), f32),
                pltpu.VMEM((share, n * ROWS, LANES), f32),
                pltpu.VMEM((n, share, ROWS, LANES), f32),
                pltpu.VMEM((2, share, ROWS, LANES), f32),
                pltpu.VMEM((4, rows, LANES), f32),
                pltpu.VMEM((n, 1, LANES), f32),
                pltpu.VMEM((n, 1, LANES), f32),
                pltpu.VMEM((2, blocks, 1, LANES), f32),
                pltpu.VMEM((2, 2 * (ehalf // LANES), LANES), f32),
                dma((4,)), dma((3,)), dma((4,)),
                dma((2, n)), dma((2, n)), dma((n,)), dma((n,)),
                dma((n,)), dma((n,)), dma((2,)),
                dma((n,)), dma((n,)), dma((n,)), dma((n,)),
                dma((2 * blocks,)), dma((2, blocks)),
                dma((2, n)), dma((2, n)), dma((2, n)), dma((2, n)), dma((2, n)), dma((2, n)),
            ],
            compiler_params=pltpu.CompilerParams(
                collective_id=0, has_side_effects=True, vmem_limit_bytes=48 * 1024 * 1024
            ),
            name="adam_step",
        )(
            kv_up_grads.reshape(n, n, ROWS, cols), tok_grads, token_rows.reshape(1, tokens), step_count,
            lines(master), lines(moment_one), lines(moment_two), lines(average),
        )
        new_kv_up, new_embed, *states = outs
        return (
            new_kv_up.reshape(owners * ROWS, cols),
            new_embed.reshape(owners * 2, width),
            *[array.reshape(1, rows * LANES) for array in states],
        )

    placed = (
        P(("group", "dp"), "mp"),
        P(("group", "dp"), None),
        P(("group", "dp")),
        P(),
        P("mp", "dp"),
        P("mp", "dp"),
        P("mp", "dp"),
        P("mp", "dp"),
    )
    return jax.shard_map(
        shards,
        mesh=mesh,
        in_specs=placed,
        out_specs=(
            P(None, "mp"),
            P("mp", None),
            P("mp", "dp"),
            P("mp", "dp"),
            P("mp", "dp"),
            P("mp", "dp"),
        ),
        check_vma=False,
    )
```

time: 1100 us -> 89.5 us (0.08)
  blocking collectives: 926 us -> 0 us
  waiting for transfers between devices: 140 us -> 0 us
  Pallas kernels: 0 us -> 77 us
  between operations: 16.9 us -> 1.3 us
    psum x2 -> x0, blocking collectives: 634 us -> none  [the longest x1 576 us: shards(): sum_squares = lax.psum(jnp.sum(gradient * gradient), ('dp', 'mp'))]
    unnamed x1 -> x0, blocking collectives: 256 us -> none
    all_gather x1 -> x0, waiting for transfers between devices: 140 us -> none  [shards(): lax.all_gather(latent_new, 'dp', axis=0, tiled=True)]
    pallas_call x0 -> x1, Pallas kernels: none -> 77 us  [shards(): pl.pallas_call(body, out_shape=(jax.ShapeDtypeStruct((n, n, ROWS, cols),...]
    all_gather x1 -> x0, blocking collectives: 36.6 us -> none  [shards(): lax.all_gather(embed_new, 'dp', axis=0, tiled=True)]
  transfers between devices with their start and end apart: 2 -> 0, of which waited for: 1 -> 0; matrix products, arithmetic and copies ran while one was open for 0% -> 0% of each run, Pallas kernels for 0% -> 0%
where the time goes in v1:
time: 89.5 us; the launch traced here: 89 us
  Pallas kernels  77 us (86%)
  local copies, waits for them, and re-layouts  10.8 us (12%)
  between operations  1.3 us (1%)
    pallas_call x1, Pallas kernels, shards(): pl.pallas_call(body, out_shape=(jax.ShapeDtypeStruct((n, n, ROWS, cols),...  77 us
    unnamed x19, local copies, waits for them, and re-layouts  9.76 us

profile of v1, /device:TPU:1, one launch (start us, length us, event | category | flops | bytes accessed | tf_op | source)
XLA Modules:
  0.0 89.0 jit_solution(17643753602913806738)
XLA Ops:
  1.3 0.0 copy-start.6
  1.3 0.7 copy-done.6
  2.0 0.0 copy-start
  2.0 1.2 %copy-done = bf16[512,1024]{1,0:T(8,128)(2,1)S(1)} copy-done((bf16[512,1024]{1,0:T(8,128)(2,1)S(1)}, bf16[512,1024]{1,0:T(8,128)(2,1)}, u32[]{:S(2)}) %copy-start) | copy-done | bytes 1048600
  3.2 0.0 copy-start.1
  3.2 1.2 %copy-done.1 = bf16[256,2048]{1,0:T(8,128)(2,1)S(1)} copy-done((bf16[256,2048]{1,0:T(8,128)(2,1)S(1)}, bf16[256,2048]{1,0:T(8,128)(2,1)}, u32[]{:S(2)}) %copy-start.1) | copy-done | bytes 1048600
  4.4 0.0 copy-start.2
  4.4 0.8 copy-done.2
  5.2 0.0 copy-start.3
  5.2 0.8 copy-done.3
  6.0 0.0 copy-start.4
  6.0 0.8 copy-done.4
  6.8 0.0 copy-start.5
  6.8 0.8 copy-done.5
  7.6 77.0 %adam_step.1 = (bf16[8,8,8,1024]{3,2,1,0:T(8,128)(2,1)S(1)}, bf16[8,8,2,2048]{3,2,1,0:T(2,128)(2,1)S(1)}, f32[96,128]{1,0:T(8,128)S(1)}, f32[96,128]{1,0:T(8,128...) custom-call(bf16[8,8,8,1024]{3,2,1,0:T(8,128)(2,1)S(1)} %bitcast.11, bf16[256,2048]{1,0:T(8,128)(2,1)S(1)} %copy-done.1, ...), custom_call_target="tpu_custom_call" | custom-call | tf_op jit(solution)/shard_map/adam_step/pallas_call | solution.py:430
  84.6 1.0 %reshape.55 = bf16[128,2048]{1,0:T(8,128)(2,1)} reshape(bf16[8,8,2,2048]{3,2,1,0:T(2,128)(2,1)S(1)} %get-tuple-element.13) | data formatting | bytes 1048576 | tf_op jit(solution)/shard_map/reshape | solution.py:471
  85.6 1.0 %copy.20 = bf16[512,1024]{1,0:T(8,128)(2,1)} copy(bf16[512,1024]{1,0:T(8,128)(2,1)S(1)} %bitcast.12) | data formatting | bytes 2097152
  86.5 0.6 copy.21
  87.2 0.6 copy.22
  87.8 0.6 copy.23
  88.4 0.6 copy.24
Async XLA Ops:
  1.3 0.7 copy-start.6
  2.0 1.2 %copy-start = (bf16[512,1024]{1,0:T(8,128)(2,1)S(1)}, bf16[512,1024]{1,0:T(8,128)(2,1)}, u32[]{:S(2)}) copy-start(bf16[512,1024]{1,0:T(8,128)(2,1)} %param.8) | copy-start | bytes 3145732
  3.2 1.2 %copy-start.1 = (bf16[256,2048]{1,0:T(8,128)(2,1)S(1)}, bf16[256,2048]{1,0:T(8,128)(2,1)}, u32[]{:S(2)}) copy-start(bf16[256,2048]{1,0:T(8,128)(2,1)} %refs_1_.1) | copy-start | bytes 3145732
  4.4 0.8 copy-start.2
  5.2 0.8 copy-start.3
  6.0 0.8 copy-start.4
  6.8 0.8 copy-start.5

commit v2 on v1

v2 whole, which is shorter than its diff:
```python
import math

import jax
import jax.numpy as jnp
import numpy as np
from jax import lax
from jax.experimental import pallas as pl
from jax.experimental.pallas import tpu as pltpu
from jax.sharding import PartitionSpec as P

BETA_ONE = 0.9
BETA_TWO = 0.95
LEARN_RATE = 0.02
DECAY_RATE = 0.1
EPSILON = 1e-08
CLIP_NORM = 1.0
AVG_DECAY = 0.9

MESH = pl.DeviceIdType.MESH
LANES = 128
ROWS = 8


def step_kernel(
    n, nx, cols, width,
    kv, tok, trow, step, master, moment_one, moment_two, average,
    okv, oem, omaster, omoment_one, omoment_two, oaverage,
    near, far, farh, hop, hop_in, toks, rows, part, enear, efar, efarh, ehop, ehop_in,
    share, share_in, grads, state, fresh, norm_a, norm_b, norm_c, wem, gkv, gem,
    state_sem, fresh_sem, tok_sem, kv_send, near_recv, far_recv, farh_recv, hop_send, hop_recv,
    em_send, enear_recv, efar_recv, efarh_recv, ehop_send, ehop_recv,
    s2_send, s2_recv, g_sem, na_send, na_recv, nb_send, nb_recv, nc_send, nc_recv,
    ga_send, ga_recv, gb_send, gb_near, gb_two, gb_fwd, gb_third, gb_four,
    ge_send, ge_near, ge_two, ge_fwd, ge_third, ge_four, gc_send, gc_recv, out_sem,
):
    group = lax.axis_index("group")
    owner = lax.axis_index("dp")
    block = lax.axis_index("mp")
    y, z = owner // n, owner % n
    other = 1 - group
    half, ehalf = cols // 2, width // 2
    chunks, echunks = half // LANES, ehalf // LANES
    one = y * other + z * group
    two = z * other + y * group
    sides = ((0, 1), (1, n - 1))

    def along_y(place):
        return place * n + z

    def along_z(place):
        return y * n + place

    def along_one(place):
        return along_y(place) * other + along_z(place) * group

    def along_two(place):
        return along_z(place) * other + along_y(place) * group

    def each(body):
        def wrapped(k, _):
            body(k)
            return 0

        lax.fori_loop(1, n, wrapped, 0)

    def near_first(i):
        return (i // 2 + 1) * (1 - i % 2) + (n - 1 - i // 2) * (i % 2)

    def in_order(body):
        def wrapped(i, _):
            body(near_first(i))
            return 0

        lax.fori_loop(0, n - 1, wrapped, 0)

    def far_first(body):
        def wrapped(i, _):
            body(near_first(n - 2 - i))
            return 0

        lax.fori_loop(0, n - 1, wrapped, 0)

    def remote(src, dst, send, recv, device):
        return pltpu.make_async_remote_copy(
            src_ref=src, dst_ref=dst, send_sem=send, recv_sem=recv, device_id=device, device_id_type=MESH
        )

    partner = (other, owner, block)

    def arrive(dst, recv):
        remote(dst, dst, g_sem.at[0], recv, partner).wait_recv()

    def land(dst, sem):
        pltpu.make_async_copy(dst, dst, sem).wait()

    states = [
        pltpu.make_async_copy(ref, state.at[i], state_sem.at[i])
        for i, ref in enumerate((master, moment_one, moment_two, average))
    ]
    ecols = pl.ds(pl.multiple_of(group * ehalf, ehalf), ehalf)
    ecols_other = pl.ds(pl.multiple_of(other * ehalf, ehalf), ehalf)
    tok_here = pltpu.make_async_copy(tok.at[:, ecols], toks.at[group], tok_sem.at[4])
    row_here = pltpu.make_async_copy(trow, rows.at[group], tok_sem.at[5])
    tok_here.start()
    row_here.start()

    barrier = pltpu.get_barrier_semaphore()

    def greet(k):
        pl.semaphore_signal(barrier, inc=1, device_id=(group, along_one((one + k) % n), block), device_id_type=MESH)
        pl.semaphore_signal(barrier, inc=1, device_id=(group, along_two((two + k) % n), block), device_id_type=MESH)

    far_first(greet)
    for k in (2, n - 2, 1, n - 1):
        pl.semaphore_signal(barrier, inc=1, device_id=(other, along_one((one + k) % n), block), device_id_type=MESH)
    for k in range(1, nx):
        for core in range(2):
            pl.semaphore_signal(barrier, inc=1, device_id=(core, owner, (block + k) % nx), device_id_type=MESH)
    pl.semaphore_signal(barrier, inc=1, device_id=partner, device_id_type=MESH)
    pl.semaphore_wait(barrier, 2 * (n - 1) + 4 + 2 * (nx - 1) + 1)

    def kv_share(h, place):
        if h == 0:
            return kv.at[place, :, :, pl.ds(0, half)]
        return kv.at[:, place, :, pl.ds(half, half)]

    def kv_part(h, place, side):
        if h == 0:
            return kv.at[place, pl.ds(side * (n // 2), n // 2), :, pl.ds(0, half)]
        return kv.at[pl.ds(side * (n // 2), n // 2), place, :, pl.ds(half, half)]

    here = (y, z)
    away = (lambda place: (0, along_y(place), block), lambda place: (1, along_z(place), block))
    out = []
    for h in range(2):
        at = here[h]
        for side, sign in sides:
            out.append(remote(
                kv_part(h, (at + 4) % n, side), farh.at[side, group],
                kv_send.at[h, side], farh_recv.at[side, group], away[h]((at + 2 * sign) % n),
            ))
    for h in range(2):
        at = here[h]
        for side, sign in sides:
            out.append(remote(
                kv_share(h, (at + 3 * sign) % n), far.at[side, group, 1],
                kv_send.at[h, 2 + side], far_recv.at[side, group, 1], away[h]((at + sign) % n),
            ))
    for copy in out:
        copy.start()
    for h in range(2):
        at = here[h]
        kept = [(far.at[side, group, 0], far_recv.at[side, group, 0], (at + 2 * sign) % n) for side, sign in sides]
        kept.append((near.at[group, 0], near_recv.at[group, 0], at))

        @pl.when(group == h)
        def _(h=h, kept=kept):
            for dst, sem, place in kept:
                pltpu.make_async_copy(kv_share(h, place), dst, sem).start()

        @pl.when(group != h)
        def _(h=h, kept=kept):
            for i, (dst, sem, place) in enumerate(kept):
                remote(kv_share(h, place), dst, kv_send.at[2, i], sem, partner).start()

    tok_there = remote(tok.at[:, ecols_other], toks.at[group], tok_sem.at[0], tok_sem.at[1], partner)
    row_there = remote(trow, rows.at[group], tok_sem.at[2], tok_sem.at[3], partner)
    tok_there.start()
    row_there.start()
    for h in range(2):
        at = here[h]
        for side, sign in sides:
            copy = remote(
                kv_share(h, (at + sign) % n), near.at[group, 1 + side],
                kv_send.at[h, 4 + side], near_recv.at[group, 1 + side], away[h]((at + sign) % n),
            )
            copy.start()
            out.append(copy)
    for copy in states:
        copy.start()

    tok_here.wait()
    row_here.wait()
    tok_there.wait_recv()
    row_there.wait_recv()
    index = lax.broadcasted_iota(jnp.int32, (2 * n * n, 1), 0)
    first, second, pair = index // (2 * n), index % n, (index // n) % 2
    yy = first * other + second * group
    zz = second * other + first * group
    wanted = block * (2 * n * n) + 2 * (yy * n + zz) + pair
    total = jnp.zeros((2 * n * n, ehalf), jnp.float32)
    for core in range(2):
        onehot = jnp.where(wanted == rows[core], 1.0, 0.0).astype(jnp.bfloat16)
        total = total + jnp.dot(onehot, toks[core], preferred_element_type=jnp.float32)
    part[...] = total.reshape(n, 2 * n, ehalf)

    def ring(place):
        return (group, along_one(place % n), block)

    eout = []
    for side, sign in sides:
        eout.append(remote(
            part.at[(one + 4) % n, pl.ds(side * n, n)], efarh.at[side],
            em_send.at[0, side], efarh_recv.at[side], ring(one + 2 * sign),
        ))
    for side, sign in sides:
        eout.append(remote(
            part.at[(one + 3 * sign) % n], efar.at[side], em_send.at[1, side], efar_recv.at[side], ring(one + sign),
        ))
    for side, sign in sides:
        eout.append(remote(
            part.at[(one + sign) % n], enear.at[side], em_send.at[2, side], enear_recv.at[side], ring(one + sign),
        ))
    for copy in eout:
        copy.start()

    hops, ehops = [], []
    for side, sign in sides:
        land(far.at[side, group, 0], far_recv.at[side, group, 0])
        arrive(far.at[side, other, 0], far_recv.at[side, other, 0])
        for core in range(2):
            arrive(far.at[side, core, 1], far_recv.at[side, core, 1])
            arrive(farh.at[side, core], farh_recv.at[side, core])
        low = side * (n // 2)

        def add_four(row, _, side=side):
            for c in range(chunks):
                span = pl.ds(c * LANES, LANES)
                acc = far[side, 0, 0, row, :, span].astype(jnp.float32)
                for core, source in ((1, 0), (0, 1), (1, 1)):
                    acc = acc + far[side, core, source, row, :, span].astype(jnp.float32)
                hop[side, row, :, span] = acc
            return 0

        def add_six(i, _, side=side, low=low):
            row = low + i
            for c in range(chunks):
                span = pl.ds(c * LANES, LANES)
                acc = far[side, 0, 0, row, :, span].astype(jnp.float32)
                for core, source in ((1, 0), (0, 1), (1, 1)):
                    acc = acc + far[side, core, source, row, :, span].astype(jnp.float32)
                for core in range(2):
                    acc = acc + farh[side, core, i, :, span].astype(jnp.float32)
                hop[side, row, :, span] = acc
            return 0

        lax.fori_loop(n // 2 - low, n - low, add_four, 0)
        lax.fori_loop(0, n // 2, add_six, 0)
        copy = remote(hop.at[side], hop_in.at[side], hop_send.at[side], hop_recv.at[side], ring(one + 2 * sign))
        copy.start()
        hops.append(copy)

    for side, sign in sides:
        arrive(efar.at[side], efar_recv.at[side])
        arrive(efarh.at[side], efarh_recv.at[side])
        to = (one + 2 * sign) % n
        for i in range(2):
            at = pl.ds(i * n, n)
            if i == side:
                ehop[side, at, :] = part[to, at, :] + efar[side, at, :] + efarh[side]
            else:
                ehop[side, at, :] = part[to, at, :] + efar[side, at, :]
        copy = remote(ehop.at[side], ehop_in.at[side], ehop_send.at[side], ehop_recv.at[side], ring(one + 2 * sign))
        copy.start()
        ehops.append(copy)

    land(near.at[group, 0], near_recv.at[group, 0])
    arrive(near.at[other, 0], near_recv.at[other, 0])
    for core in range(2):
        for side in range(2):
            arrive(near.at[core, 1 + side], near_recv.at[core, 1 + side])

    def add_near(row, _):
        at = pl.ds(pl.multiple_of(row * ROWS, ROWS), ROWS)
        for c in range(chunks):
            span = pl.ds(c * LANES, LANES)
            acc = near[0, 0, row, :, span].astype(jnp.float32)
            for core, source in ((1, 0), (0, 1), (1, 1), (0, 2), (1, 2)):
                acc = acc + near[core, source, row, :, span].astype(jnp.float32)
            share[c, at, :] = acc
        return 0

    lax.fori_loop(0, n, add_near, 0)
    for side in range(2):
        arrive(enear.at[side], enear_recv.at[side])
    enear[0] = part[one] + enear[0] + enear[1]
    for side in range(2):
        arrive(hop_in.at[side], hop_recv.at[side])

    def add_hops(row, _):
        at = pl.ds(pl.multiple_of(row * ROWS, ROWS), ROWS)
        for c in range(chunks):
            span = pl.ds(c * LANES, LANES)
            share[c, at, :] = share[c, at, :] + hop_in[0, row, :, span] + hop_in[1, row, :, span]
        return 0

    lax.fori_loop(0, n, add_hops, 0)
    for side in range(2):
        arrive(ehop_in.at[side], ehop_recv.at[side])
    for c in range(echunks):
        span = pl.ds(c * LANES, LANES)
        for i in range(2):
            at = pl.ds(i * n, n)
            piece = enear[0, at, span] + ehop_in[0, at, span] + ehop_in[1, at, span]
            share[chunks + i, pl.ds(c, n, stride=ROWS), :] = piece

    def send_share(k):
        place = (two + k) % n
        return remote(
            share.at[:, pl.ds(pl.multiple_of(place * ROWS, ROWS), ROWS), :],
            share_in.at[two], s2_send.at[k], s2_recv.at[two], (group, along_two(place), block),
        )

    far_first(lambda k: send_share(k).start())
    share_in[two] = share[:, pl.ds(pl.multiple_of(two * ROWS, ROWS), ROWS), :]

    def wait_share(k):
        place = (two + k) % n
        arrive(share_in.at[place], s2_recv.at[place])

    in_order(wait_share)
    mine = share_in[0]
    for place in range(1, n):
        mine = mine + share_in[place]
    grads[group] = mine
    swap = remote(grads.at[group], grads.at[group], g_sem.at[0], g_sem.at[1], partner)
    swap.start()

    squares = mine * mine
    lanes = squares[0]
    for c in range(1, chunks + 2):
        lanes = lanes + squares[c]
    norm_a[y] = jnp.sum(lanes, axis=0, keepdims=True)

    def send_a(k):
        place = (y + k) % n
        return remote(norm_a.at[y], norm_a.at[y], na_send.at[k], na_recv.at[y], (group, along_y(place), block))

    def wait_a(k):
        place = (y + k) % n
        arrive(norm_a.at[place], na_recv.at[place])

    far_first(lambda k: send_a(k).start())
    in_order(wait_a)
    partial = norm_a[0]
    for place in range(1, n):
        partial = partial + norm_a[place]
    norm_b[z] = partial

    def send_b(k):
        place = (z + k) % n
        return remote(norm_b.at[z], norm_b.at[z], nb_send.at[k], nb_recv.at[z], (group, along_z(place), block))

    def wait_b(k):
        place = (z + k) % n
        arrive(norm_b.at[place], nb_recv.at[place])

    far_first(lambda k: send_b(k).start())
    in_order(wait_b)
    partial = norm_b[0]
    for place in range(1, n):
        partial = partial + norm_b[place]
    norm_c[group, block] = partial

    def send_c(k, core):
        place = (block + k) % nx
        to = group if core == 0 else other
        slot = 2 * k + core
        return remote(
            norm_c.at[group, block], norm_c.at[group, block], nc_send.at[slot], nc_recv.at[group, block], (to, owner, place)
        )

    fan = [(k, core) for k in range(nx) for core in range(2) if k or core]
    for k, core in fan:
        send_c(k, core).start()
    for k, core in fan:
        place = (block + k) % nx
        source = group if core == 0 else other
        arrive(norm_c.at[source, place], nc_recv.at[source, place])
    partial = jnp.zeros((1, LANES), jnp.float32)
    for core in range(2):
        for place in range(nx):
            partial = partial + norm_c[core, place]
    norm_value = jnp.sqrt(jnp.sum(partial, axis=1, keepdims=True))
    factor = CLIP_NORM / jnp.maximum(norm_value, CLIP_NORM)

    swap.wait_recv()
    for copy in states:
        copy.wait()

    step_float = jnp.full((1, LANES), step[0], jnp.int32).astype(jnp.float32)
    one_scale = 1.0 - jnp.exp(step_float * math.log(np.float32(BETA_ONE)))
    two_scale = 1.0 - jnp.exp(step_float * math.log(np.float32(BETA_TWO)))

    def update(at, gradient):
        clipped = factor * gradient
        weight = state[0, at, :]
        new_one = BETA_ONE * state[1, at, :] + (1.0 - BETA_ONE) * clipped
        new_two = BETA_TWO * state[2, at, :] + (1.0 - BETA_TWO) * clipped * clipped
        first_hat = new_one / one_scale
        second_hat = new_two / two_scale
        new_weight = weight - LEARN_RATE * (first_hat / (jnp.sqrt(second_hat) + EPSILON) + DECAY_RATE * weight)
        fresh[0, at, :] = new_weight
        fresh[1, at, :] = new_one
        fresh[2, at, :] = new_two
        fresh[3, at, :] = AVG_DECAY * state[3, at, :] + (1.0 - AVG_DECAY) * new_weight
        return new_weight

    row_chunks = cols // LANES
    for h in range(2):
        for c in range(chunks):
            span = pl.ds(h * half + c * LANES, LANES)
            new = update(pl.ds(h * chunks + c, ROWS, stride=row_chunks), grads[h, c])

            @pl.when(group == h)
            def _(new=new, span=span):
                gkv[y, z, :, span] = new.astype(jnp.bfloat16)

        for i in range(2):
            at = pl.ds(ROWS * row_chunks + (i * 2 + h) * echunks, echunks)
            wem[h, pl.ds(i * echunks, echunks), :] = update(at, grads[h, chunks + i, 0:echunks, :])

    for c in range(echunks):
        for h in range(2):
            @pl.when(group == h)
            def _(h=h, c=c):
                gem[y, z, :, pl.ds(h * ehalf + c * LANES, LANES)] = wem[h, pl.ds(c, 2, stride=echunks), :].astype(jnp.bfloat16)

    kcols = pl.ds(pl.multiple_of(group * half, half), half)

    def block_of(ref, place_one, place_two, span):
        return ref.at[place_one * other + place_two * group, place_two * other + place_one * group, :, span]

    def gather_one(ref, span, kind, k):
        place = (one + k) % n
        mine = block_of(ref, one, two, span)
        return remote(mine, mine, ga_send.at[kind, k], ga_recv.at[kind, one], (group, along_one(place), block))

    def came_one(ref, span, kind, place):
        arrive(block_of(ref, place, two, span), ga_recv.at[kind, place])

    def second(place):
        return (group, along_two(place % n), block)

    def spread(place):
        ref = block_of(gkv, place, two, kcols)
        for side, sign in sides:
            remote(ref, ref, gb_send.at[1, side], gb_two.at[side, place], second(two + 2 * sign)).start()
        for side, sign in sides:
            remote(ref, ref, gb_send.at[0, side], gb_near.at[side], second(two + sign)).start()

    def half_cols(side):
        return pl.ds(pl.multiple_of(group * half + side * (half // 2), half // 2), half // 2)

    def forward(place):
        for side, sign in sides:
            source = (two - 2 * sign + 2 * n) % n
            ref = block_of(gkv, place, source, kcols)
            arrive(ref, gb_two.at[side, place])
            remote(ref, ref, gb_fwd.at[0, side], gb_third.at[side], second(two + sign)).start()
            ref = block_of(gkv, place, source, half_cols(side))
            remote(ref, ref, gb_fwd.at[1, side], gb_four.at[side], second(two + 2 * sign)).start()

    def line(ref, core, place, side=None):
        wide = ref.shape[3] // 2
        span = pl.ds(core * wide, wide) if side is None else pl.ds(core * wide + side * (wide // 2), wide // 2)
        return ref.at[:, place, :, span] if core == 0 else ref.at[place, :, :, span]

    far_first(lambda k: gather_one(gkv, kcols, 0, k).start())
    far_first(lambda k: gather_one(gem, ecols, 1, k).start())
    spread(one)

    def relay(k):
        place = (one + k) % n
        came_one(gkv, kcols, 0, place)
        spread(place)

    in_order(relay)
    in_order(lambda k: came_one(gem, ecols, 1, (one + k) % n))

    results = ((0, gkv, okv), (1, gem, oem))
    for i, ref in enumerate((omaster, omoment_one, omoment_two, oaverage)):
        pltpu.make_async_copy(fresh.at[i], ref, fresh_sem.at[i]).start()

    for core in range(2):
        @pl.when(group == core)
        def _(core=core):
            def hand_over(place):
                for kind, ref, result in results:
                    mine = line(ref, core, place)
                    remote(mine, mine, gc_send.at[kind, place], gc_recv.at[kind, place], partner).start()
                    pltpu.make_async_copy(mine, line(result, core, place), out_sem.at[core, kind, place]).start()

            mine = line(gem, core, two)
            for side, sign in sides:
                remote(mine, mine, ge_send.at[1, side], ge_two.at[side], second(two + 2 * sign)).start()
            for side, sign in sides:
                remote(mine, mine, ge_send.at[0, side], ge_near.at[side], second(two + sign)).start()
            hand_over(two)
            forward(one)
            in_order(lambda k: forward((one + k) % n))
            for side, sign in sides:
                source = (two - 2 * sign + 2 * n) % n
                ref = line(gem, core, source)
                arrive(ref, ge_two.at[side])
                remote(ref, ref, ge_fwd.at[0, side], ge_third.at[side], second(two + sign)).start()
                ref = line(gem, core, source, side)
                remote(ref, ref, ge_fwd.at[1, side], ge_four.at[side], second(two + 2 * sign)).start()
            for side, sign in sides:
                source = (two - sign + n) % n
                arrive(line(gkv, core, source), gb_near.at[side])
                arrive(line(gem, core, source), ge_near.at[side])
                hand_over(source)
            for side, sign in sides:
                hand_over((two - 2 * sign + 2 * n) % n)
            for side, sign in sides:
                source = (two - 3 * sign + 3 * n) % n
                arrive(line(gkv, core, source), gb_third.at[side])
                arrive(line(gem, core, source), ge_third.at[side])
                hand_over(source)
            source = (two + 4) % n
            for side, sign in sides:
                arrive(line(gkv, core, source, side), gb_four.at[side])
                arrive(line(gem, core, source, side), ge_four.at[side])
            hand_over(source)

            def take(place, _):
                for kind, ref, result in results:
                    theirs = line(ref, 1 - core, place)
                    arrive(theirs, gc_recv.at[kind, place])
                    pltpu.make_async_copy(theirs, line(result, 1 - core, place), out_sem.at[1 - core, kind, place]).start()
                return 0

            lax.fori_loop(0, n, take, 0)

            def sent_lines(place, _):
                for kind, ref, result in results:
                    mine = line(ref, core, place)
                    remote(mine, mine, gc_send.at[kind, place], gc_recv.at[kind, place], partner).wait_send()
                    for h in range(2):
                        pltpu.make_async_copy(line(ref, h, place), line(result, h, place), out_sem.at[h, kind, place]).wait()
                return 0

            lax.fori_loop(0, n, sent_lines, 0)
            for side in range(2):
                for i in range(2):
                    for ref, sends in ((gkv, gb_send), (gem, ge_send)):
                        mine = line(ref, core, two)
                        remote(mine, mine, sends.at[i, side], g_sem.at[1], partner).wait_send()
                for ref, sends in ((gkv, gb_fwd), (gem, ge_fwd)):
                    mine = line(ref, core, two)
                    remote(mine, mine, sends.at[0, side], g_sem.at[1], partner).wait_send()
                    mine = line(ref, core, two, side)
                    remote(mine, mine, sends.at[1, side], g_sem.at[1], partner).wait_send()

    for copy in out + eout + hops + ehops:
        copy.wait_send()
    for i in range(3):
        remote(near.at[0, 0], near.at[0, 0], kv_send.at[2, i], g_sem.at[1], partner).wait_send()
    tok_there.wait_send()
    row_there.wait_send()
    swap.wait_send()

    def sent(k):
        send_share(k).wait_send()
        send_a(k).wait_send()
        send_b(k).wait_send()
        gather_one(gkv, kcols, 0, k).wait_send()
        gather_one(gem, ecols, 1, k).wait_send()

    each(sent)
    for k, core in fan:
        send_c(k, core).wait_send()
    for i, ref in enumerate((omaster, omoment_one, omoment_two, oaverage)):
        pltpu.make_async_copy(fresh.at[i], ref, fresh_sem.at[i]).wait()


def write_out(kv, em, *refs):
    states, (okv, oem), out_states = refs[:4], refs[4:6], refs[6:10]
    kv_in, em_in, em_out, state_in, read, write = refs[10:]
    pieces = kv_in.shape[0]
    cut = kv.shape[0] // pieces
    plan = [(kv.at[pl.ds(i * cut, cut)], kv_in.at[i], okv.at[pl.ds(i * cut, cut)]) for i in range(pieces)]
    plan += [(states[i], state_in.at[i], out_states[i]) for i in range(4)]
    plan += [(em, em_in, None)]
    reads = [pltpu.make_async_copy(src, mid, read.at[i]) for i, (src, mid, _) in enumerate(plan)]
    for copy in reads:
        copy.start()
    writes = []
    for i, (_, mid, dst) in enumerate(plan):
        reads[i].wait()
        if dst is not None:
            writes.append(pltpu.make_async_copy(mid, dst, write.at[i]))
            writes[-1].start()
        else:
            rows, width = em_out.shape
            for row in range(0, rows, 8):
                em_out[row:row + 8, :] = em_in[row // 2:row // 2 + 4].reshape(8, width)
            writes.append(pltpu.make_async_copy(em_out, oem, write.at[i]))
            writes[-1].start()
    for copy in writes:
        copy.wait()


def solution(mesh):
    owners, blocks = mesh.shape["dp"], mesh.shape["mp"]
    n = math.isqrt(owners)

    def shards(kv_up_grads, tok_grads, token_rows, step_count, master, moment_one, moment_two, average):
        cols, width, tokens = kv_up_grads.shape[1], tok_grads.shape[1], tok_grads.shape[0]
        rows = master.shape[1] // LANES
        half, ehalf = cols // 2, width // 2
        lines = lambda array: array.reshape(rows, LANES)
        dma, f32, bf16 = pltpu.SemaphoreType.DMA, jnp.float32, jnp.bfloat16
        any_space = pl.BlockSpec(memory_space=pltpu.HBM)
        state = jax.ShapeDtypeStruct((rows, LANES), f32)
        share = half // LANES + 2

        def body(*refs):
            step_kernel(n, blocks, cols, width, *refs)

        outs = pl.pallas_call(
            body,
            out_shape=(
                jax.ShapeDtypeStruct((n, n, ROWS, cols), bf16),
                jax.ShapeDtypeStruct((n, n, 2, width), bf16),
                state, state, state, state,
            ),
            in_specs=[any_space] * 3 + [pl.BlockSpec(memory_space=pltpu.SMEM)] + [any_space] * 4,
            out_specs=[any_space] * 6,
            scratch_shapes=[
                pltpu.VMEM((2, 3, n, ROWS, half), bf16),
                pltpu.VMEM((2, 2, 2, n, ROWS, half), bf16),
                pltpu.VMEM((2, 2, n // 2, ROWS, half), bf16),
                pltpu.VMEM((2, n, ROWS, half), f32),
                pltpu.VMEM((2, n, ROWS, half), f32),
                pltpu.VMEM((2, tokens, ehalf), bf16),
                pltpu.VMEM((2, 1, tokens), jnp.int32),
                pltpu.VMEM((n, 2 * n, ehalf), f32),
                pltpu.VMEM((2, 2 * n, ehalf), f32),
                pltpu.VMEM((2, 2 * n, ehalf), f32),
                pltpu.VMEM((2, n, ehalf), f32),
                pltpu.VMEM((2, 2 * n, ehalf), f32),
                pltpu.VMEM((2, 2 * n, ehalf), f32),
                pltpu.VMEM((share, n * ROWS, LANES), f32),
                pltpu.VMEM((n, share, ROWS, LANES), f32),
                pltpu.VMEM((2, share, ROWS, LANES), f32),
                pltpu.VMEM((4, rows, LANES), f32),
                pltpu.VMEM((4, rows, LANES), f32),
                pltpu.VMEM((n, 1, LANES), f32),
                pltpu.VMEM((n, 1, LANES), f32),
                pltpu.VMEM((2, blocks, 1, LANES), f32),
                pltpu.VMEM((2, 2 * (ehalf // LANES), LANES), f32),
                pltpu.VMEM((n, n, ROWS, cols), bf16),
                pltpu.VMEM((n, n, 2, width), bf16),
                dma((4,)), dma((4,)), dma((6,)),
                dma((3, 6)), dma((2, 3)), dma((2, 2, 2)), dma((2, 2)), dma((2,)), dma((2,)),
                dma((3, 2)), dma((2,)), dma((2,)), dma((2,)), dma((2,)), dma((2,)),
                dma((n,)), dma((n,)), dma((2,)),
                dma((n,)), dma((n,)), dma((n,)), dma((n,)),
                dma((2 * blocks,)), dma((2, blocks)),
                dma((2, n)), dma((2, n)),
                dma((2, 2)), dma((2,)), dma((2, n)), dma((2, 2)), dma((2,)), dma((2,)),
                dma((2, 2)), dma((2,)), dma((2,)), dma((2, 2)), dma((2,)), dma((2,)),
                dma((2, n)), dma((2, n)), dma((2, 2, n)),
            ],
            compiler_params=pltpu.CompilerParams(
                collective_id=0, has_side_effects=True
            ),
            name="adam_step",
        )(
            kv_up_grads.reshape(n, n, ROWS, cols), tok_grads, token_rows.reshape(1, tokens), step_count,
            lines(master), lines(moment_one), lines(moment_two), lines(average),
        )
        new_kv_up, new_embed, *states = outs
        new_kv_up, new_embed, *states = pl.pallas_call(
            write_out,
            out_shape=(
                jax.ShapeDtypeStruct(new_kv_up.shape, bf16), jax.ShapeDtypeStruct((owners * 2, width), bf16),
                state, state, state, state,
            ),
            in_specs=[any_space] * 6,
            out_specs=[any_space] * 6,
            scratch_shapes=[
                pltpu.VMEM((4, n // 4, n, ROWS, cols), bf16),
                pltpu.VMEM((owners, 2, width), bf16),
                pltpu.VMEM((owners * 2, width), bf16),
                pltpu.VMEM((4, rows, LANES), f32),
                dma((9,)), dma((9,)),
            ],
            name="write_out",
        )(new_kv_up, new_embed.reshape(owners, 2, width), *states)
        return (
            new_kv_up.reshape(owners * ROWS, cols),
            new_embed,
            *[array.reshape(1, rows * LANES) for array in states],
        )

    placed = (
        P(("group", "dp"), "mp"),
        P(("group", "dp"), None),
        P(("group", "dp")),
        P(),
        P("mp", "dp"),
        P("mp", "dp"),
        P("mp", "dp"),
        P("mp", "dp"),
    )
    return jax.shard_map(
        shards,
        mesh=mesh,
        in_specs=placed,
        out_specs=(
            P(None, "mp"),
            P("mp", None),
            P("mp", "dp"),
            P("mp", "dp"),
            P("mp", "dp"),
            P("mp", "dp"),
        ),
        check_vma=False,
    )
```

time: 89.5 us -> 69.4 us (0.78)
  local copies, waits for them, and re-layouts: 10.8 us -> 0 us
  Pallas kernels: 77 us -> 67.9 us
    pallas_call x1, Pallas kernels: 77 us -> 65.5 us  [shards(): pl.pallas_call(body, out_shape=(jax.ShapeDtypeStruct((n, n, ROWS, cols),...]
    unnamed x19 -> x0, local copies, waits for them, and re-layouts: 9.76 us -> none
    pallas_call x0 -> x1, Pallas kernels: none -> 2.44 us  [shards(): pl.pallas_call(write_out, out_shape=(jax.ShapeDtypeStruct(new_kv_up.shape...]
    reshape x1 -> x0, local copies, waits for them, and re-layouts: 0.99 us -> none  [shards(): new_embed.reshape(owners * 2, width)]
where the time goes in v2:
time: 69.4 us; the launch traced here: 69.2 us
  Pallas kernels  67.9 us (98%)
  between operations  1.29 us (2%)
    pallas_call x1, Pallas kernels, shards(): pl.pallas_call(body, out_shape=(jax.ShapeDtypeStruct((n, n, ROWS, cols),...  65.5 us
    pallas_call x1, Pallas kernels, shards(): pl.pallas_call(write_out, out_shape=(jax.ShapeDtypeStruct(new_kv_up.shape...  2.44 us

profile of v2, /device:TPU:1, one launch (start us, length us, event | category | flops | bytes accessed | tf_op | source)
XLA Modules:
  0.0 69.2 jit_solution(17777553837265018136)
XLA Ops:
  1.3 65.5 %adam_step.1 = (bf16[8,8,8,1024]{3,2,1,0:T(8,128)(2,1)}, bf16[8,8,2,2048]{3,2,1,0:T(2,128)(2,1)}, f32[96,128]{1,0:T(8,128)}, f32[96,128]{1,0:T(8,128)}, f32[96,128]{1,0:T(8,128)}, /*index=5*/f32[96,128]{1,0:T(8,128)}) custom-call(bf16[8,8,8,1024]{3,2,1,0:T(8,128)(2,1)} %bitcast.12, bf16[256,2048]{1,0:T(8,128)(2,1)} %refs_1_.1, s32[1,256]{1,0:T(1,128)} %bitcast.18, ...), custom_call_target="tpu_custom_call" | custom-call | tf_op jit(solution)/shard_map/adam_step/pallas_call | solution.py:622
  66.8 2.4 %write_out.1 = (bf16[8,8,8,1024]{3,2,1,0:T(8,128)(2,1)}, bf16[128,2048]{1,0:T(8,128)(2,1)}, f32[96,128]{1,0:T(8,128)}, f32[96,128]{1,0:T(8,128)}, f32[96,128]{1,0:T(8,128)}, /*index=5*/f32[96,128]{1,0:T(8,128)}) custom-call(bf16[8,8,8,1024]{3,2,1,0:T(8,128)(2,1)} %get-tuple-element.18.kv, bf16[64,2,2048]{2,1,0:T(2,128)(2,1)} %bitcast.13, ...), custom_call_target="tpu_custom_call" | custom-call | tf_op jit(solution)/shard_map/write_out/pallas_call | solution.py:676

commit v3 on v2

--- a/solution.py
+++ b/solution.py
@@ -24,14 +24,14 @@
 def step_kernel(
     n, nx, cols, width,
     kv, tok, trow, step, master, moment_one, moment_two, average,
-    okv, oem, omaster, omoment_one, omoment_two, oaverage,
+    gkv, gem, omaster, omoment_one, omoment_two, oaverage,
     near, far, farh, hop, hop_in, toks, rows, part, enear, efar, efarh, ehop, ehop_in,
-    share, share_in, grads, state, fresh, norm_a, norm_b, norm_c, wem, gkv, gem,
-    state_sem, fresh_sem, tok_sem, kv_send, near_recv, far_recv, farh_recv, hop_send, hop_recv,
+    share, share_in, grads, state, norm_a, norm_b, norm_c, wem,
+    state_sem, tok_sem, kv_send, near_recv, far_recv, farh_recv, hop_send, hop_recv,
     em_send, enear_recv, efar_recv, efarh_recv, ehop_send, ehop_recv,
     s2_send, s2_recv, g_sem, na_send, na_recv, nb_send, nb_recv, nc_send, nc_recv,
     ga_send, ga_recv, gb_send, gb_near, gb_two, gb_fwd, gb_third, gb_four,
-    ge_send, ge_near, ge_two, ge_fwd, ge_third, ge_four, gc_send, gc_recv, out_sem,
+    ge_send, ge_near, ge_two, ge_fwd, ge_third, ge_four, gc_send, gc_recv,
 ):
     group = lax.axis_index("group")
     owner = lax.axis_index("dp")
@@ -295,6 +295,17 @@
         return 0
 
     lax.fori_loop(0, n, add_hops, 0)
+
+    spans = (pl.ds(0, chunks), pl.ds(chunks, 2))
+
+    def send_share(kind, k):
+        place = (two + k) % n
+        return remote(
+            share.at[spans[kind], pl.ds(pl.multiple_of(place * ROWS, ROWS), ROWS), :],
+            share_in.at[two, spans[kind]], s2_send.at[kind, k], s2_recv.at[kind, two], (group, along_two(place), block),
+        )
+
+    far_first(lambda k: send_share(0, k).start())
     for side in range(2):
         arrive(ehop_in.at[side], ehop_recv.at[side])
     for c in range(echunks):
@@ -304,19 +315,13 @@
             piece = enear[0, at, span] + ehop_in[0, at, span] + ehop_in[1, at, span]
             share[chunks + i, pl.ds(c, n, stride=ROWS), :] = piece
 
-    def send_share(k):
-        place = (two + k) % n
-        return remote(
-            share.at[:, pl.ds(pl.multiple_of(place * ROWS, ROWS), ROWS), :],
-            share_in.at[two], s2_send.at[k], s2_recv.at[two], (group, along_two(place), block),
-        )
-
-    far_first(lambda k: send_share(k).start())
+    far_first(lambda k: send_share(1, k).start())
     share_in[two] = share[:, pl.ds(pl.multiple_of(two * ROWS, ROWS), ROWS), :]
 
     def wait_share(k):
         place = (two + k) % n
-        arrive(share_in.at[place], s2_recv.at[place])
+        for kind in range(2):
+            arrive(share_in.at[place, spans[kind]], s2_recv.at[kind, place])
 
     in_order(wait_share)
     mine = share_in[0]
@@ -400,10 +405,10 @@
         first_hat = new_one / one_scale
         second_hat = new_two / two_scale
         new_weight = weight - LEARN_RATE * (first_hat / (jnp.sqrt(second_hat) + EPSILON) + DECAY_RATE * weight)
-        fresh[0, at, :] = new_weight
-        fresh[1, at, :] = new_one
-        fresh[2, at, :] = new_two
-        fresh[3, at, :] = AVG_DECAY * state[3, at, :] + (1.0 - AVG_DECAY) * new_weight
+        omaster[at, :] = new_weight
+        omoment_one[at, :] = new_one
+        omoment_two[at, :] = new_two
+        oaverage[at, :] = AVG_DECAY * state[3, at, :] + (1.0 - AVG_DECAY) * new_weight
         return new_weight
 
     row_chunks = cols // LANES
@@ -478,18 +483,14 @@
     in_order(relay)
     in_order(lambda k: came_one(gem, ecols, 1, (one + k) % n))
 
-    results = ((0, gkv, okv), (1, gem, oem))
-    for i, ref in enumerate((omaster, omoment_one, omoment_two, oaverage)):
-        pltpu.make_async_copy(fresh.at[i], ref, fresh_sem.at[i]).start()
-
+    results = ((0, gkv), (1, gem))
     for core in range(2):
         @pl.when(group == core)
         def _(core=core):
             def hand_over(place):
-                for kind, ref, result in results:
+                for kind, ref in results:
                     mine = line(ref, core, place)
                     remote(mine, mine, gc_send.at[kind, place], gc_recv.at[kind, place], partner).start()
-                    pltpu.make_async_copy(mine, line(result, core, place), out_sem.at[core, kind, place]).start()
 
             mine = line(gem, core, two)
             for side, sign in sides:
@@ -525,20 +526,17 @@
             hand_over(source)
 
             def take(place, _):
-                for kind, ref, result in results:
+                for kind, ref in results:
                     theirs = line(ref, 1 - core, place)
                     arrive(theirs, gc_recv.at[kind, place])
-                    pltpu.make_async_copy(theirs, line(result, 1 - core, place), out_sem.at[1 - core, kind, place]).start()
                 return 0
 
             lax.fori_loop(0, n, take, 0)
 
             def sent_lines(place, _):
-                for kind, ref, result in results:
+                for kind, ref in results:
                     mine = line(ref, core, place)
                     remote(mine, mine, gc_send.at[kind, place], gc_recv.at[kind, place], partner).wait_send()
-                    for h in range(2):
-                        pltpu.make_async_copy(line(ref, h, place), line(result, h, place), out_sem.at[h, kind, place]).wait()
                 return 0
 
             lax.fori_loop(0, n, sent_lines, 0)
@@ -562,7 +560,8 @@
     swap.wait_send()
 
     def sent(k):
-        send_share(k).wait_send()
+        send_share(0, k).wait_send()
+        send_share(1, k).wait_send()
         send_a(k).wait_send()
         send_b(k).wait_send()
         gather_one(gkv, kcols, 0, k).wait_send()
@@ -571,33 +570,21 @@
     each(sent)
     for k, core in fan:
         send_c(k, core).wait_send()
-    for i, ref in enumerate((omaster, omoment_one, omoment_two, oaverage)):
-        pltpu.make_async_copy(fresh.at[i], ref, fresh_sem.at[i]).wait()
 
 
 def write_out(kv, em, *refs):
-    states, (okv, oem), out_states = refs[:4], refs[4:6], refs[6:10]
-    kv_in, em_in, em_out, state_in, read, write = refs[10:]
-    pieces = kv_in.shape[0]
-    cut = kv.shape[0] // pieces
-    plan = [(kv.at[pl.ds(i * cut, cut)], kv_in.at[i], okv.at[pl.ds(i * cut, cut)]) for i in range(pieces)]
-    plan += [(states[i], state_in.at[i], out_states[i]) for i in range(4)]
-    plan += [(em, em_in, None)]
-    reads = [pltpu.make_async_copy(src, mid, read.at[i]) for i, (src, mid, _) in enumerate(plan)]
-    for copy in reads:
+    states, (okv, oem), out_states, em_out, sem = refs[:4], refs[4:6], refs[6:10], refs[10], refs[11]
+    writes = [pltpu.make_async_copy(kv, okv, sem.at[0])]
+    writes += [pltpu.make_async_copy(states[i], out_states[i], sem.at[1 + i]) for i in range(4)]
+    for copy in writes:
         copy.start()
-    writes = []
-    for i, (_, mid, dst) in enumerate(plan):
-        reads[i].wait()
-        if dst is not None:
-            writes.append(pltpu.make_async_copy(mid, dst, write.at[i]))
-            writes[-1].start()
-        else:
-            rows, width = em_out.shape
-            for row in range(0, rows, 8):
-                em_out[row:row + 8, :] = em_in[row // 2:row // 2 + 4].reshape(8, width)
-            writes.append(pltpu.make_async_copy(em_out, oem, write.at[i]))
-            writes[-1].start()
+    rows, width = em_out.shape
+    cut = rows // 4
+    for i in range(4):
+        for row in range(i * cut, (i + 1) * cut, 8):
+            em_out[row:row + 8, :] = em[row // 2:row // 2 + 4].reshape(8, width)
+        writes.append(pltpu.make_async_copy(em_out.at[pl.ds(i * cut, cut)], oem.at[pl.ds(i * cut, cut)], sem.at[5 + i]))
+        writes[-1].start()
     for copy in writes:
         copy.wait()
 
@@ -613,6 +600,8 @@
         lines = lambda array: array.reshape(rows, LANES)
         dma, f32, bf16 = pltpu.SemaphoreType.DMA, jnp.float32, jnp.bfloat16
         any_space = pl.BlockSpec(memory_space=pltpu.HBM)
+        vmem = pl.BlockSpec(memory_space=pltpu.VMEM)
+        stay = lambda array: pltpu.with_memory_space_constraint(array, pltpu.HBM)
         state = jax.ShapeDtypeStruct((rows, LANES), f32)
         share = half // LANES + 2
 
@@ -627,7 +616,7 @@
                 state, state, state, state,
             ),
             in_specs=[any_space] * 3 + [pl.BlockSpec(memory_space=pltpu.SMEM)] + [any_space] * 4,
-            out_specs=[any_space] * 6,
+            out_specs=[vmem] * 6,
             scratch_shapes=[
                 pltpu.VMEM((2, 3, n, ROWS, half), bf16),
                 pltpu.VMEM((2, 2, 2, n, ROWS, half), bf16),
@@ -646,31 +635,28 @@
                 pltpu.VMEM((n, share, ROWS, LANES), f32),
                 pltpu.VMEM((2, share, ROWS, LANES), f32),
                 pltpu.VMEM((4, rows, LANES), f32),
-                pltpu.VMEM((4, rows, LANES), f32),
                 pltpu.VMEM((n, 1, LANES), f32),
                 pltpu.VMEM((n, 1, LANES), f32),
                 pltpu.VMEM((2, blocks, 1, LANES), f32),
                 pltpu.VMEM((2, 2 * (ehalf // LANES), LANES), f32),
-                pltpu.VMEM((n, n, ROWS, cols), bf16),
-                pltpu.VMEM((n, n, 2, width), bf16),
-                dma((4,)), dma((4,)), dma((6,)),
+                dma((4,)), dma((6,)),
                 dma((3, 6)), dma((2, 3)), dma((2, 2, 2)), dma((2, 2)), dma((2,)), dma((2,)),
                 dma((3, 2)), dma((2,)), dma((2,)), dma((2,)), dma((2,)), dma((2,)),
-                dma((n,)), dma((n,)), dma((2,)),
+                dma((2, n)), dma((2, n)), dma((2,)),
                 dma((n,)), dma((n,)), dma((n,)), dma((n,)),
                 dma((2 * blocks,)), dma((2, blocks)),
                 dma((2, n)), dma((2, n)),
                 dma((2, 2)), dma((2,)), dma((2, n)), dma((2, 2)), dma((2,)), dma((2,)),
                 dma((2, 2)), dma((2,)), dma((2,)), dma((2, 2)), dma((2,)), dma((2,)),
-                dma((2, n)), dma((2, n)), dma((2, 2, n)),
+                dma((2, n)), dma((2, n)),
             ],
             compiler_params=pltpu.CompilerParams(
-                collective_id=0, has_side_effects=True
+                collective_id=0, has_side_effects=True, vmem_limit_bytes=48 * 1024 * 1024
             ),
             name="adam_step",
         )(
-            kv_up_grads.reshape(n, n, ROWS, cols), tok_grads, token_rows.reshape(1, tokens), step_count,
-            lines(master), lines(moment_one), lines(moment_two), lines(average),
+            stay(kv_up_grads.reshape(n, n, ROWS, cols)), stay(tok_grads), stay(token_rows.reshape(1, tokens)), step_count,
+            stay(lines(master)), stay(lines(moment_one)), stay(lines(moment_two)), stay(lines(average)),
         )
         new_kv_up, new_embed, *states = outs
         new_kv_up, new_embed, *states = pl.pallas_call(
@@ -679,15 +665,10 @@
                 jax.ShapeDtypeStruct(new_kv_up.shape, bf16), jax.ShapeDtypeStruct((owners * 2, width), bf16),
                 state, state, state, state,
             ),
-            in_specs=[any_space] * 6,
+            in_specs=[vmem] * 6,
             out_specs=[any_space] * 6,
-            scratch_shapes=[
-                pltpu.VMEM((4, n // 4, n, ROWS, cols), bf16),
-                pltpu.VMEM((owners, 2, width), bf16),
-                pltpu.VMEM((owners * 2, width), bf16),
-                pltpu.VMEM((4, rows, LANES), f32),
-                dma((9,)), dma((9,)),
-            ],
+            scratch_shapes=[pltpu.VMEM((owners * 2, width), bf16), dma((9,))],
+            compiler_params=pltpu.CompilerParams(vmem_limit_bytes=16 * 1024 * 1024),
             name="write_out",
         )(new_kv_up, new_embed.reshape(owners, 2, width), *states)
         return (

time: 69.4 us -> 65.9 us (0.950)
  Pallas kernels: 67.9 us -> 64.5 us
    pallas_call x1, Pallas kernels: 65.5 us -> 63.3 us  [shards(): pl.pallas_call(body, out_shape=(jax.ShapeDtypeStruct((n, n, ROWS, cols),...]
    pallas_call x1, Pallas kernels: 2.44 us -> 1.28 us  [shards(): pl.pallas_call(write_out, out_shape=(jax.ShapeDtypeStruct(new_kv_up.shape...]
where the time goes in v3:
time: 65.9 us; the launch traced here: 65.8 us
  Pallas kernels  64.5 us (98%)
  between operations  1.29 us (2%)
    pallas_call x1, Pallas kernels, shards(): pl.pallas_call(body, out_shape=(jax.ShapeDtypeStruct((n, n, ROWS, cols),...  63.3 us

profile of v3, /device:TPU:1, one launch (start us, length us, event | category | flops | bytes accessed | tf_op | source)
XLA Modules:
  0.0 65.8 jit_solution(12352338928963133017)
XLA Ops:
  1.3 63.3 %adam_step.1 = (bf16[8,8,8,1024]{3,2,1,0:T(8,128)(2,1)S(1)}, bf16[8,8,2,2048]{3,2,1,0:T(2,128)(2,1)S(1)}, f32[96,128]{1,0:T(8,128)S(1)}, f32[96,128]{1,0:T(8,128...) custom-call(bf16[8,8,8,1024]{3,2,1,0:T(8,128)(2,1)} %bitcast.13, bf16[256,2048]{1,0:T(8,128)(2,1)} %refs_1_.1, ...), custom_call_target="tpu_custom_call" | custom-call | tf_op jit(solution)/shard_map/adam_step/pallas_call | solution.py:611
  64.5 1.3 %write_out.1 = (bf16[8,8,8,1024]{3,2,1,0:T(8,128)(2,1)}, bf16[128,2048]{1,0:T(8,128)(2,1)}, f32[96,128]{1,0:T(8,128)}, f32[96,128]{1,0:T(8,128)}, f32[96,128]{1,0:T(8,128)}, /*index=5*/f32[96,128]{1,0:T(8,128)}) custom-call(bf16[8,8,8,1024]{3,2,1,0:T(8,128)(2,1)S(1)} %get-tuple-element.18.kv, bf16[64,2,2048]{2,1,0:T(2,128)(2,1)S(1)} %bitcast.12, ...), custom_call_target="tpu_custom_call" | custom-call | tf_op jit(solution)/shard_map/write_out/pallas_call | solution.py:662

commit v4 on v3

--- a/solution.py
+++ b/solution.py
@@ -31,7 +31,7 @@
     em_send, enear_recv, efar_recv, efarh_recv, ehop_send, ehop_recv,
     s2_send, s2_recv, g_sem, na_send, na_recv, nb_send, nb_recv, nc_send, nc_recv,
     ga_send, ga_recv, gb_send, gb_near, gb_two, gb_fwd, gb_third, gb_four,
-    ge_send, ge_near, ge_two, ge_fwd, ge_third, ge_four, gc_send, gc_recv,
+    ge_send, ge_near, ge_two, ge_fwd, ge_third, ge_four, gc_send, gc_recv, known,
 ):
     group = lax.axis_index("group")
     owner = lax.axis_index("dp")
@@ -104,32 +104,38 @@
     tok_here.start()
     row_here.start()
 
+    def kv_share(h, place):
+        if h == 0:
+            return kv.at[place, :, :, pl.ds(0, half)]
+        return kv.at[:, place, :, pl.ds(half, half)]
+
+    def kv_part(h, place, side):
+        if h == 0:
+            return kv.at[place, pl.ds(side * (n // 2), n // 2), :, pl.ds(0, half)]
+        return kv.at[pl.ds(side * (n // 2), n // 2), place, :, pl.ds(half, half)]
+
+    here = (y, z)
+    kept = []
+    for h in range(2):
+        at = here[h]
+        kept.append([(far.at[side, group, 0], far_recv.at[side, group, 0], (at + 2 * sign) % n) for side, sign in sides])
+        kept[h].append((near.at[group, 0], near_recv.at[group, 0], at))
+
+        @pl.when(group == h)
+        def _(h=h):
+            for dst, sem, place in kept[h]:
+                pltpu.make_async_copy(kv_share(h, place), dst, sem).start()
+
     barrier = pltpu.get_barrier_semaphore()
-
-    def greet(k):
-        pl.semaphore_signal(barrier, inc=1, device_id=(group, along_one((one + k) % n), block), device_id_type=MESH)
-        pl.semaphore_signal(barrier, inc=1, device_id=(group, along_two((two + k) % n), block), device_id_type=MESH)
-
-    far_first(greet)
     for k in (2, n - 2, 1, n - 1):
-        pl.semaphore_signal(barrier, inc=1, device_id=(other, along_one((one + k) % n), block), device_id_type=MESH)
+        for core in (group, other):
+            pl.semaphore_signal(barrier, inc=1, device_id=(core, along_one((one + k) % n), block), device_id_type=MESH)
     for k in range(1, nx):
         for core in range(2):
             pl.semaphore_signal(barrier, inc=1, device_id=(core, owner, (block + k) % nx), device_id_type=MESH)
     pl.semaphore_signal(barrier, inc=1, device_id=partner, device_id_type=MESH)
-    pl.semaphore_wait(barrier, 2 * (n - 1) + 4 + 2 * (nx - 1) + 1)
-
-    def kv_share(h, place):
-        if h == 0:
-            return kv.at[place, :, :, pl.ds(0, half)]
-        return kv.at[:, place, :, pl.ds(half, half)]
-
-    def kv_part(h, place, side):
-        if h == 0:
-            return kv.at[place, pl.ds(side * (n // 2), n // 2), :, pl.ds(0, half)]
-        return kv.at[pl.ds(side * (n // 2), n // 2), place, :, pl.ds(half, half)]
-
-    here = (y, z)
+    pl.semaphore_wait(barrier, 8 + 2 * (nx - 1) + 1)
+
     away = (lambda place: (0, along_y(place), block), lambda place: (1, along_z(place), block))
     out = []
     for h in range(2):
@@ -149,18 +155,9 @@
     for copy in out:
         copy.start()
     for h in range(2):
-        at = here[h]
-        kept = [(far.at[side, group, 0], far_recv.at[side, group, 0], (at + 2 * sign) % n) for side, sign in sides]
-        kept.append((near.at[group, 0], near_recv.at[group, 0], at))
-
-        @pl.when(group == h)
-        def _(h=h, kept=kept):
-            for dst, sem, place in kept:
-                pltpu.make_async_copy(kv_share(h, place), dst, sem).start()
-
         @pl.when(group != h)
-        def _(h=h, kept=kept):
-            for i, (dst, sem, place) in enumerate(kept):
+        def _(h=h):
+            for i, (dst, sem, place) in enumerate(kept[h]):
                 remote(kv_share(h, place), dst, kv_send.at[2, i], sem, partner).start()
 
     tok_there = remote(tok.at[:, ecols_other], toks.at[group], tok_sem.at[0], tok_sem.at[1], partner)
@@ -286,6 +283,7 @@
     enear[0] = part[one] + enear[0] + enear[1]
     for side in range(2):
         arrive(hop_in.at[side], hop_recv.at[side])
+    pl.semaphore_signal(known, inc=1, device_id=partner, device_id_type=MESH)
 
     def add_hops(row, _):
         at = pl.ds(pl.multiple_of(row * ROWS, ROWS), ROWS)
@@ -305,6 +303,7 @@
             share_in.at[two, spans[kind]], s2_send.at[kind, k], s2_recv.at[kind, two], (group, along_two(place), block),
         )
 
+    pl.semaphore_wait(known, 1)
     far_first(lambda k: send_share(0, k).start())
     for side in range(2):
         arrive(ehop_in.at[side], ehop_recv.at[side])
@@ -346,6 +345,12 @@
         arrive(norm_a.at[place], na_recv.at[place])
 
     far_first(lambda k: send_a(k).start())
+    for copy in out + eout + hops + ehops:
+        copy.wait_send()
+    for i in range(3):
+        remote(near.at[0, 0], near.at[0, 0], kv_send.at[2, i], g_sem.at[1], partner).wait_send()
+    tok_there.wait_send()
+    row_there.wait_send()
     in_order(wait_a)
     partial = norm_a[0]
     for place in range(1, n):
@@ -361,6 +366,12 @@
         arrive(norm_b.at[place], nb_recv.at[place])
 
     far_first(lambda k: send_b(k).start())
+    for kind in range(2):
+        each(lambda k: send_share(kind, k).wait_send())
+    each(lambda k: send_a(k).wait_send())
+    swap.wait()
+    for copy in states:
+        copy.wait()
     in_order(wait_b)
     partial = norm_b[0]
     for place in range(1, n):
@@ -378,6 +389,10 @@
     fan = [(k, core) for k in range(nx) for core in range(2) if k or core]
     for k, core in fan:
         send_c(k, core).start()
+    each(lambda k: send_b(k).wait_send())
+    step_float = jnp.full((1, LANES), step[0], jnp.int32).astype(jnp.float32)
+    one_scale = 1.0 - jnp.exp(step_float * math.log(np.float32(BETA_ONE)))
+    two_scale = 1.0 - jnp.exp(step_float * math.log(np.float32(BETA_TWO)))
     for k, core in fan:
         place = (block + k) % nx
         source = group if core == 0 else other
@@ -388,14 +403,6 @@
             partial = partial + norm_c[core, place]
     norm_value = jnp.sqrt(jnp.sum(partial, axis=1, keepdims=True))
     factor = CLIP_NORM / jnp.maximum(norm_value, CLIP_NORM)
-
-    swap.wait_recv()
-    for copy in states:
-        copy.wait()
-
-    step_float = jnp.full((1, LANES), step[0], jnp.int32).astype(jnp.float32)
-    one_scale = 1.0 - jnp.exp(step_float * math.log(np.float32(BETA_ONE)))
-    two_scale = 1.0 - jnp.exp(step_float * math.log(np.float32(BETA_TWO)))
 
     def update(at, gradient):
         clipped = factor * gradient
@@ -487,8 +494,8 @@
     for core in range(2):
         @pl.when(group == core)
         def _(core=core):
-            def hand_over(place):
-                for kind, ref in results:
+            def hand_over(place, kinds=results):
+                for kind, ref in kinds:
                     mine = line(ref, core, place)
                     remote(mine, mine, gc_send.at[kind, place], gc_recv.at[kind, place], partner).start()
 
@@ -497,7 +504,10 @@
                 remote(mine, mine, ge_send.at[1, side], ge_two.at[side], second(two + 2 * sign)).start()
             for side, sign in sides:
                 remote(mine, mine, ge_send.at[0, side], ge_near.at[side], second(two + sign)).start()
-            hand_over(two)
+            each(lambda k: gather_one(gkv, kcols, 0, k).wait_send())
+            each(lambda k: gather_one(gem, ecols, 1, k).wait_send())
+            for k, to in fan:
+                send_c(k, to).wait_send()
             forward(one)
             in_order(lambda k: forward((one + k) % n))
             for side, sign in sides:
@@ -507,6 +517,7 @@
                 remote(ref, ref, ge_fwd.at[0, side], ge_third.at[side], second(two + sign)).start()
                 ref = line(gem, core, source, side)
                 remote(ref, ref, ge_fwd.at[1, side], ge_four.at[side], second(two + 2 * sign)).start()
+            hand_over(two)
             for side, sign in sides:
                 source = (two - sign + n) % n
                 arrive(line(gkv, core, source), gb_near.at[side])
@@ -514,16 +525,17 @@
                 hand_over(source)
             for side, sign in sides:
                 hand_over((two - 2 * sign + 2 * n) % n)
-            for side, sign in sides:
-                source = (two - 3 * sign + 3 * n) % n
-                arrive(line(gkv, core, source), gb_third.at[side])
-                arrive(line(gem, core, source), ge_third.at[side])
-                hand_over(source)
-            source = (two + 4) % n
-            for side, sign in sides:
-                arrive(line(gkv, core, source, side), gb_four.at[side])
-                arrive(line(gem, core, source, side), ge_four.at[side])
-            hand_over(source)
+            last = (two + 4) % n
+            for kind in range(2):
+                ref = results[kind][1]
+                third, four = ((gb_third, gb_four), (ge_third, ge_four))[kind]
+                for side, sign in sides:
+                    source = (two - 3 * sign + 3 * n) % n
+                    arrive(line(ref, core, source), third.at[side])
+                    hand_over(source, results[kind:kind + 1])
+                for side in range(2):
+                    arrive(line(ref, core, last, side), four.at[side])
+                hand_over(last, results[kind:kind + 1])
 
             def take(place, _):
                 for kind, ref in results:
@@ -550,26 +562,6 @@
                     remote(mine, mine, sends.at[0, side], g_sem.at[1], partner).wait_send()
                     mine = line(ref, core, two, side)
                     remote(mine, mine, sends.at[1, side], g_sem.at[1], partner).wait_send()
-
-    for copy in out + eout + hops + ehops:
-        copy.wait_send()
-    for i in range(3):
-        remote(near.at[0, 0], near.at[0, 0], kv_send.at[2, i], g_sem.at[1], partner).wait_send()
-    tok_there.wait_send()
-    row_there.wait_send()
-    swap.wait_send()
-
-    def sent(k):
-        send_share(0, k).wait_send()
-        send_share(1, k).wait_send()
-        send_a(k).wait_send()
-        send_b(k).wait_send()
-        gather_one(gkv, kcols, 0, k).wait_send()
-        gather_one(gem, ecols, 1, k).wait_send()
-
-    each(sent)
-    for k, core in fan:
-        send_c(k, core).wait_send()
 
 
 def write_out(kv, em, *refs):
@@ -648,7 +640,7 @@
                 dma((2, n)), dma((2, n)),
                 dma((2, 2)), dma((2,)), dma((2, n)), dma((2, 2)), dma((2,)), dma((2,)),
                 dma((2, 2)), dma((2,)), dma((2,)), dma((2, 2)), dma((2,)), dma((2,)),
-                dma((2, n)), dma((2, n)),
+                dma((2, n)), dma((2, n)), pltpu.SemaphoreType.REGULAR,
             ],
             compiler_params=pltpu.CompilerParams(
                 collective_id=0, has_side_effects=True, vmem_limit_bytes=48 * 1024 * 1024

time: 65.9 us -> 66.2 us (level)
  no operation moved by 1% of the time
where the time goes in v4:
time: 66.2 us; the launch traced here: 66 us
  Pallas kernels  64.7 us (98%)
  between operations  1.29 us (2%)
    pallas_call x1, Pallas kernels, shards(): pl.pallas_call(body, out_shape=(jax.ShapeDtypeStruct((n, n, ROWS, cols),...  63.5 us

profile of v4, /device:TPU:1, one launch (start us, length us, event | category | flops | bytes accessed | tf_op | source)
XLA Modules:
  0.0 66.0 jit_solution(9286557485212232112)
XLA Ops:
  1.3 63.5 %adam_step.1 = (bf16[8,8,8,1024]{3,2,1,0:T(8,128)(2,1)S(1)}, bf16[8,8,2,2048]{3,2,1,0:T(2,128)(2,1)S(1)}, f32[96,128]{1,0:T(8,128)S(1)}, f32[96,128]{1,0:T(8,128...) custom-call(bf16[8,8,8,1024]{3,2,1,0:T(8,128)(2,1)} %bitcast.13, bf16[256,2048]{1,0:T(8,128)(2,1)} %refs_1_.1, ...), custom_call_target="tpu_custom_call" | custom-call | tf_op jit(solution)/shard_map/adam_step/pallas_call | solution.py:603
  64.7 1.3 %write_out.1 = (bf16[8,8,8,1024]{3,2,1,0:T(8,128)(2,1)}, bf16[128,2048]{1,0:T(8,128)(2,1)}, f32[96,128]{1,0:T(8,128)}, f32[96,128]{1,0:T(8,128)}, f32[96,128]{1,0:T(8,128)}, /*index=5*/f32[96,128]{1,0:T(8,128)}) custom-call(bf16[8,8,8,1024]{3,2,1,0:T(8,128)(2,1)S(1)} %get-tuple-element.18.kv, bf16[64,2,2048]{2,1,0:T(2,128)(2,1)S(1)} %bitcast.12, ...), custom_call_target="tpu_custom_call" | custom-call | tf_op jit(solution)/shard_map/write_out/pallas_call | solution.py:654

commit v5 on v4

--- a/solution.py
+++ b/solution.py
@@ -26,11 +26,11 @@
     kv, tok, trow, step, master, moment_one, moment_two, average,
     gkv, gem, omaster, omoment_one, omoment_two, oaverage,
     near, far, farh, hop, hop_in, toks, rows, part, enear, efar, efarh, ehop, ehop_in,
-    share, share_in, grads, state, norm_a, norm_b, norm_c, wem,
+    share, share_in, grads, state, lstate, lgrads, norm_a, norm_b, norm_c, wem,
     state_sem, tok_sem, kv_send, near_recv, far_recv, farh_recv, hop_send, hop_recv,
     em_send, enear_recv, efar_recv, efarh_recv, ehop_send, ehop_recv,
     s2_send, s2_recv, g_sem, na_send, na_recv, nb_send, nb_recv, nc_send, nc_recv,
-    ga_send, ga_recv, gb_send, gb_near, gb_two, gb_fwd, gb_third, gb_four,
+    ls_send, ls_recv, lg_send, lg_recv, gb_send, gb_near, gb_two, gb_fwd, gb_third, gb_four,
     ge_send, ge_near, ge_two, ge_fwd, ge_third, ge_four, gc_send, gc_recv, known,
 ):
     group = lax.axis_index("group")
@@ -305,6 +305,29 @@
 
     pl.semaphore_wait(known, 1)
     far_first(lambda k: send_share(0, k).start())
+
+    row_chunks = cols // LANES
+    for copy in states:
+        copy.wait()
+
+    def place_of(h, t):
+        if t < chunks:
+            return pl.ds(h * chunks + t, ROWS, stride=row_chunks)
+        return pl.ds(ROWS * row_chunks + ((t - chunks) * 2 + h) * echunks, echunks)
+
+    for h in range(2):
+        @pl.when(group == h)
+        def _(h=h):
+            for a in range(3):
+                for t in range(chunks + 2):
+                    lstate[one, a, t] = state[a, place_of(h, t), :]
+
+    def send_state(a, k):
+        return remote(lstate.at[one, a], lstate.at[one, a], ls_send.at[a, k], ls_recv.at[a, one], ring(one + k))
+
+    def send_grads(k):
+        return remote(lgrads.at[one], lgrads.at[one], lg_send.at[k], lg_recv.at[one], ring(one + k))
+
     for side in range(2):
         arrive(ehop_in.at[side], ehop_recv.at[side])
     for c in range(echunks):
@@ -315,6 +338,7 @@
             share[chunks + i, pl.ds(c, n, stride=ROWS), :] = piece
 
     far_first(lambda k: send_share(1, k).start())
+    far_first(lambda k: send_state(0, k).start())
     share_in[two] = share[:, pl.ds(pl.multiple_of(two * ROWS, ROWS), ROWS), :]
 
     def wait_share(k):
@@ -327,6 +351,7 @@
     for place in range(1, n):
         mine = mine + share_in[place]
     grads[group] = mine
+    lgrads[one] = mine
     swap = remote(grads.at[group], grads.at[group], g_sem.at[0], g_sem.at[1], partner)
     swap.start()
 
@@ -345,6 +370,8 @@
         arrive(norm_a.at[place], na_recv.at[place])
 
     far_first(lambda k: send_a(k).start())
+    far_first(lambda k: send_grads(k).start())
+    far_first(lambda k: send_state(1, k).start())
     for copy in out + eout + hops + ehops:
         copy.wait_send()
     for i in range(3):
@@ -366,12 +393,11 @@
         arrive(norm_b.at[place], nb_recv.at[place])
 
     far_first(lambda k: send_b(k).start())
+    far_first(lambda k: send_state(2, k).start())
     for kind in range(2):
         each(lambda k: send_share(kind, k).wait_send())
     each(lambda k: send_a(k).wait_send())
     swap.wait()
-    for copy in states:
-        copy.wait()
     in_order(wait_b)
     partial = norm_b[0]
     for place in range(1, n):
@@ -404,52 +430,29 @@
     norm_value = jnp.sqrt(jnp.sum(partial, axis=1, keepdims=True))
     factor = CLIP_NORM / jnp.maximum(norm_value, CLIP_NORM)
 
-    def update(at, gradient):
+    def moments(gradient, old_one, old_two):
         clipped = factor * gradient
-        weight = state[0, at, :]
-        new_one = BETA_ONE * state[1, at, :] + (1.0 - BETA_ONE) * clipped
-        new_two = BETA_TWO * state[2, at, :] + (1.0 - BETA_TWO) * clipped * clipped
+        new_one = BETA_ONE * old_one + (1.0 - BETA_ONE) * clipped
+        new_two = BETA_TWO * old_two + (1.0 - BETA_TWO) * clipped * clipped
+        return new_one, new_two
+
+    def weight_after(weight, new_one, new_two):
         first_hat = new_one / one_scale
         second_hat = new_two / two_scale
-        new_weight = weight - LEARN_RATE * (first_hat / (jnp.sqrt(second_hat) + EPSILON) + DECAY_RATE * weight)
-        omaster[at, :] = new_weight
-        omoment_one[at, :] = new_one
-        omoment_two[at, :] = new_two
-        oaverage[at, :] = AVG_DECAY * state[3, at, :] + (1.0 - AVG_DECAY) * new_weight
-        return new_weight
-
-    row_chunks = cols // LANES
-    for h in range(2):
-        for c in range(chunks):
-            span = pl.ds(h * half + c * LANES, LANES)
-            new = update(pl.ds(h * chunks + c, ROWS, stride=row_chunks), grads[h, c])
-
-            @pl.when(group == h)
-            def _(new=new, span=span):
-                gkv[y, z, :, span] = new.astype(jnp.bfloat16)
-
-        for i in range(2):
-            at = pl.ds(ROWS * row_chunks + (i * 2 + h) * echunks, echunks)
-            wem[h, pl.ds(i * echunks, echunks), :] = update(at, grads[h, chunks + i, 0:echunks, :])
-
-    for c in range(echunks):
-        for h in range(2):
-            @pl.when(group == h)
-            def _(h=h, c=c):
-                gem[y, z, :, pl.ds(h * ehalf + c * LANES, LANES)] = wem[h, pl.ds(c, 2, stride=echunks), :].astype(jnp.bfloat16)
+        return weight - LEARN_RATE * (first_hat / (jnp.sqrt(second_hat) + EPSILON) + DECAY_RATE * weight)
+
+    def come(k):
+        place = (one + k) % n
+        for a in range(3):
+            arrive(lstate.at[place, a], ls_recv.at[a, place])
+        arrive(lgrads.at[place], lg_recv.at[place])
+
+    each(come)
 
     kcols = pl.ds(pl.multiple_of(group * half, half), half)
 
     def block_of(ref, place_one, place_two, span):
         return ref.at[place_one * other + place_two * group, place_two * other + place_one * group, :, span]
-
-    def gather_one(ref, span, kind, k):
-        place = (one + k) % n
-        mine = block_of(ref, one, two, span)
-        return remote(mine, mine, ga_send.at[kind, k], ga_recv.at[kind, one], (group, along_one(place), block))
-
-    def came_one(ref, span, kind, place):
-        arrive(block_of(ref, place, two, span), ga_recv.at[kind, place])
 
     def second(place):
         return (group, along_two(place % n), block)
@@ -478,17 +481,47 @@
         span = pl.ds(core * wide, wide) if side is None else pl.ds(core * wide + side * (wide // 2), wide // 2)
         return ref.at[:, place, :, span] if core == 0 else ref.at[place, :, :, span]
 
-    far_first(lambda k: gather_one(gkv, kcols, 0, k).start())
-    far_first(lambda k: gather_one(gem, ecols, 1, k).start())
-    spread(one)
-
-    def relay(k):
-        place = (one + k) % n
-        came_one(gkv, kcols, 0, place)
+    def make(place):
+        new = []
+        for t in range(chunks + 2):
+            new_one, new_two = moments(lgrads[place, t], lstate[place, 1, t], lstate[place, 2, t])
+            new.append(weight_after(lstate[place, 0, t], new_one, new_two))
+        for i in range(2):
+            wem[pl.ds(i * echunks, echunks), :] = new[chunks + i][0:echunks]
+        at = (place * other + two * group, two * other + place * group)
+        for h in range(2):
+            @pl.when(group == h)
+            def _(h=h):
+                for t in range(chunks):
+                    gkv[at[0], at[1], :, pl.ds(h * half + t * LANES, LANES)] = new[t].astype(jnp.bfloat16)
+                for c in range(echunks):
+                    span = pl.ds(h * ehalf + c * LANES, LANES)
+                    gem[at[0], at[1], :, span] = wem[pl.ds(c, 2, stride=echunks), :].astype(jnp.bfloat16)
+
         spread(place)
 
-    in_order(relay)
-    in_order(lambda k: came_one(gem, ecols, 1, (one + k) % n))
+    def make_all(place, _):
+        make(place)
+        return 0
+
+    lax.fori_loop(0, n, make_all, 0)
+
+    def keep_own():
+        for h in range(2):
+            for t in range(chunks + 2):
+                at = place_of(h, t)
+                weight = state[0, at, :]
+                new_one, new_two = moments(grads[h, t], state[1, at, :], state[2, at, :])
+                new_weight = weight_after(weight, new_one, new_two)
+                omaster[at, :] = new_weight
+                omoment_one[at, :] = new_one
+                omoment_two[at, :] = new_two
+                oaverage[at, :] = AVG_DECAY * state[3, at, :] + (1.0 - AVG_DECAY) * new_weight
+        for a in range(3):
+            each(lambda k: send_state(a, k).wait_send())
+        each(lambda k: send_grads(k).wait_send())
+        for k, to in fan:
+            send_c(k, to).wait_send()
 
     results = ((0, gkv), (1, gem))
     for core in range(2):
@@ -504,12 +537,13 @@
                 remote(mine, mine, ge_send.at[1, side], ge_two.at[side], second(two + 2 * sign)).start()
             for side, sign in sides:
                 remote(mine, mine, ge_send.at[0, side], ge_near.at[side], second(two + sign)).start()
-            each(lambda k: gather_one(gkv, kcols, 0, k).wait_send())
-            each(lambda k: gather_one(gem, ecols, 1, k).wait_send())
-            for k, to in fan:
-                send_c(k, to).wait_send()
-            forward(one)
-            in_order(lambda k: forward((one + k) % n))
+            keep_own()
+
+            def forward_all(place, _):
+                forward(place)
+                return 0
+
+            lax.fori_loop(0, n, forward_all, 0)
             for side, sign in sides:
                 source = (two - 2 * sign + 2 * n) % n
                 ref = line(gem, core, source)
@@ -627,17 +661,19 @@
                 pltpu.VMEM((n, share, ROWS, LANES), f32),
                 pltpu.VMEM((2, share, ROWS, LANES), f32),
                 pltpu.VMEM((4, rows, LANES), f32),
+                pltpu.VMEM((n, 3, share, ROWS, LANES), f32),
+                pltpu.VMEM((n, share, ROWS, LANES), f32),
                 pltpu.VMEM((n, 1, LANES), f32),
                 pltpu.VMEM((n, 1, LANES), f32),
                 pltpu.VMEM((2, blocks, 1, LANES), f32),
-                pltpu.VMEM((2, 2 * (ehalf // LANES), LANES), f32),
+                pltpu.VMEM((2 * (ehalf // LANES), LANES), f32),
                 dma((4,)), dma((6,)),
                 dma((3, 6)), dma((2, 3)), dma((2, 2, 2)), dma((2, 2)), dma((2,)), dma((2,)),
                 dma((3, 2)), dma((2,)), dma((2,)), dma((2,)), dma((2,)), dma((2,)),
                 dma((2, n)), dma((2, n)), dma((2,)),
                 dma((n,)), dma((n,)), dma((n,)), dma((n,)),
                 dma((2 * blocks,)), dma((2, blocks)),
-                dma((2, n)), dma((2, n)),
+                dma((3, n)), dma((3, n)), dma((n,)), dma((n,)),
                 dma((2, 2)), dma((2,)), dma((2, n)), dma((2, 2)), dma((2,)), dma((2,)),
                 dma((2, 2)), dma((2,)), dma((2,)), dma((2, 2)), dma((2,)), dma((2,)),
                 dma((2, n)), dma((2, n)), pltpu.SemaphoreType.REGULAR,

time: 66.2 us -> 64.6 us (0.976)
  Pallas kernels: 64.7 us -> 63.2 us
    pallas_call x1, Pallas kernels: 63.5 us -> 61.9 us  [shards(): pl.pallas_call(body, out_shape=(jax.ShapeDtypeStruct((n, n, ROWS, cols),...]
where the time goes in v5:
time: 64.6 us; the launch traced here: 64.5 us
  Pallas kernels  63.2 us (98%)
  between operations  1.29 us (2%)
    pallas_call x1, Pallas kernels, shards(): pl.pallas_call(body, out_shape=(jax.ShapeDtypeStruct((n, n, ROWS, cols),...  61.9 us

profile of v5, /device:TPU:1, one launch (start us, length us, event | category | flops | bytes accessed | tf_op | source)
XLA Modules:
  0.0 64.5 jit_solution(659325234088570293)
XLA Ops:
  1.3 61.9 %adam_step.1 = (bf16[8,8,8,1024]{3,2,1,0:T(8,128)(2,1)S(1)}, bf16[8,8,2,2048]{3,2,1,0:T(2,128)(2,1)S(1)}, f32[96,128]{1,0:T(8,128)S(1)}, f32[96,128]{1,0:T(8,128...) custom-call(bf16[8,8,8,1024]{3,2,1,0:T(8,128)(2,1)} %bitcast.13, bf16[256,2048]{1,0:T(8,128)(2,1)} %refs_1_.1, ...), custom_call_target="tpu_custom_call" | custom-call | tf_op jit(solution)/shard_map/adam_step/pallas_call | solution.py:637
  63.2 1.3 %write_out.1 = (bf16[8,8,8,1024]{3,2,1,0:T(8,128)(2,1)}, bf16[128,2048]{1,0:T(8,128)(2,1)}, f32[96,128]{1,0:T(8,128)}, f32[96,128]{1,0:T(8,128)}, f32[96,128]{1,0:T(8,128)}, /*index=5*/f32[96,128]{1,0:T(8,128)}) custom-call(bf16[8,8,8,1024]{3,2,1,0:T(8,128)(2,1)S(1)} %get-tuple-element.18.kv, bf16[64,2,2048]{2,1,0:T(2,128)(2,1)S(1)} %bitcast.12, ...), custom_call_target="tpu_custom_call" | custom-call | tf_op jit(solution)/shard_map/write_out/pallas_call | solution.py:690

commit v6 on v5

--- a/solution.py
+++ b/solution.py
@@ -461,8 +461,6 @@
         ref = block_of(gkv, place, two, kcols)
         for side, sign in sides:
             remote(ref, ref, gb_send.at[1, side], gb_two.at[side, place], second(two + 2 * sign)).start()
-        for side, sign in sides:
-            remote(ref, ref, gb_send.at[0, side], gb_near.at[side], second(two + sign)).start()
 
     def half_cols(side):
         return pl.ds(pl.multiple_of(group * half + side * (half // 2), half // 2), half // 2)
@@ -536,9 +534,9 @@
             for side, sign in sides:
                 remote(mine, mine, ge_send.at[1, side], ge_two.at[side], second(two + 2 * sign)).start()
             for side, sign in sides:
-                remote(mine, mine, ge_send.at[0, side], ge_near.at[side], second(two + sign)).start()
-            keep_own()
-
+                for ref, sends, comes in ((gkv, gb_send, gb_near), (gem, ge_send, ge_near)):
+                    mine = line(ref, core, two)
+                    remote(mine, mine, sends.at[0, side], comes.at[side], second(two + sign)).start()
             def forward_all(place, _):
                 forward(place)
                 return 0
@@ -552,6 +550,7 @@
                 ref = line(gem, core, source, side)
                 remote(ref, ref, ge_fwd.at[1, side], ge_four.at[side], second(two + 2 * sign)).start()
             hand_over(two)
+            keep_own()
             for side, sign in sides:
                 source = (two - sign + n) % n
                 arrive(line(gkv, core, source), gb_near.at[side])

time: 64.6 us -> 64 us (level)
  no operation moved by 1% of the time
where the time goes in v6:
time: 64 us; the launch traced here: 63.9 us
  Pallas kernels  62.6 us (98%)
  between operations  1.29 us (2%)
    pallas_call x1, Pallas kernels, shards(): pl.pallas_call(body, out_shape=(jax.ShapeDtypeStruct((n, n, ROWS, cols),...  61.3 us

profile of v6, /device:TPU:1, one launch (start us, length us, event | category | flops | bytes accessed | tf_op | source)
XLA Modules:
  0.0 63.9 jit_solution(481182715915445479)
XLA Ops:
  1.3 61.3 %adam_step.1 = (bf16[8,8,8,1024]{3,2,1,0:T(8,128)(2,1)S(1)}, bf16[8,8,2,2048]{3,2,1,0:T(2,128)(2,1)S(1)}, f32[96,128]{1,0:T(8,128)S(1)}, f32[96,128]{1,0:T(8,128...) custom-call(bf16[8,8,8,1024]{3,2,1,0:T(8,128)(2,1)} %bitcast.13, bf16[256,2048]{1,0:T(8,128)(2,1)} %refs_1_.1, ...), custom_call_target="tpu_custom_call" | custom-call | tf_op jit(solution)/shard_map/adam_step/pallas_call | solution.py:636
  62.6 1.3 %write_out.1 = (bf16[8,8,8,1024]{3,2,1,0:T(8,128)(2,1)}, bf16[128,2048]{1,0:T(8,128)(2,1)}, f32[96,128]{1,0:T(8,128)}, f32[96,128]{1,0:T(8,128)}, f32[96,128]{1,0:T(8,128)}, /*index=5*/f32[96,128]{1,0:T(8,128)}) custom-call(bf16[8,8,8,1024]{3,2,1,0:T(8,128)(2,1)S(1)} %get-tuple-element.18.kv, bf16[64,2,2048]{2,1,0:T(2,128)(2,1)S(1)} %bitcast.12, ...), custom_call_target="tpu_custom_call" | custom-call | tf_op jit(solution)/shard_map/write_out/pallas_call | solution.py:689
